TPU v7x, 128 devices: a whole 4x4x4 slice. The times are simulated.
128 devices in a mesh: row: 32 (over y_lo, z, x), col: 4 (over y_hi, core).
Axes of the slice: x: 4, y: 4 (y_hi: 2, y_lo: 2; y = y_hi * 2 + y_lo), z: 4, core: 2. Of those that a mesh axis runs over, the one named last changes fastest.
Arguments:
- flow: bfloat16 [8192, 8192], P('row', 'col'), may hold values from 0.0009994507 to 1
- pattern: int32 [32, 32], P('row', 'col'), may hold values 0 or 1
- keep: int32 [32, 32], P('row', 'col'), may hold values 0 or 1
Outputs:
- clustered: float32 [8192, 8192], P('row', 'col')
All inputs are finite; a program needn't handle non-finite values. No bound on the sum of `pattern` or of `keep` on one device may be relied on, other than what follows from the above.
Results may differ from a plain program's by a relative error of at most 0.00046.
Values may be sent and summed in bfloat16 or wider, within the bound.
A program may use at most 128 MiB of HBM per device.

v0:
```python
import jax
import jax.numpy as jnp
from jax import lax
from jax.sharding import PartitionSpec as P


def spread_tiles(grid, tile):
    trows, tcols = grid.shape
    wide = jnp.broadcast_to(grid[:, None, :, None], (trows, tile, tcols, tile))
    return wide.reshape(trows * tile, tcols * tile)


def body(flow, pattern, keep):
    rows_dev, cols_dev = flow.shape
    trows, tcols = pattern.shape
    tile = rows_dev // trows
    row_start = lax.axis_index("row") * rows_dev
    col_start = lax.axis_index("col") * cols_dev
    global_rows = row_start + lax.iota(jnp.int32, rows_dev)
    global_cols = col_start + lax.iota(jnp.int32, cols_dev)
    loops = (global_rows[:, None] == global_cols[None, :]).astype(jnp.float32)
    base = flow.astype(jnp.float32) * spread_tiles((pattern > 0).astype(jnp.float32), tile) + loops
    mass = lax.psum(jnp.sum(base, axis=0), "row")
    stochastic = (base / mass[None, :]).astype(jnp.bfloat16)
    left = lax.all_gather(stochastic, "col", axis=1, tiled=True)
    right = lax.all_gather(stochastic, "row", axis=0, tiled=True)
    expanded = jnp.dot(left, right, preferred_element_type=jnp.float32)
    tile_rows = lax.axis_index("row") * trows + lax.iota(jnp.int32, trows)
    tile_cols = lax.axis_index("col") * tcols + lax.iota(jnp.int32, tcols)
    kept = jnp.logical_or(keep > 0, tile_rows[:, None] == tile_cols[None, :]).astype(jnp.float32)
    expanded = expanded * spread_tiles(kept, tile)
    inflated = expanded * expanded
    partial_totals = jnp.sum(inflated, axis=0)
    order = rows_dev * lax.axis_size("row")
    totals = lax.psum(partial_totals, "row")
    scale = order / totals
    return inflated * scale[None, :]


def solution(mesh):
    return jax.shard_map(
        body,
        mesh=mesh,
        in_specs=(P("row", "col"), P("row", "col"), P("row", "col")),
        out_specs=P("row", "col"),
        check_vma=False,
    )
```

profile of v0, /device:TPU:0, one launch (start us, length us, event | category | flops | bytes accessed | tf_op | source)
XLA Modules:
  0.0 601.0 jit_solution(7701374311171810818)
XLA Ops:
  6.5 0.0 all-gather.3.cloned.1.call-start
  6.5 0.7 fusion.2
  7.2 0.1 broadcast_bitcast_fusion.1
  7.3 1.7 fusion.1
  9.0 85.2 %psum.14 = f32[2048]{0:T(1024)S(1)} all-reduce(f32[2048]{0:T(1024)S(1)} %fusion.1), channel_id=1, replica_groups=mesh['row'=32,'col'=4] {'row'}, use_global_device_ids=true, to_apply=%region_1.0 | all-reduce | flops 2048 | bytes 16384 | tf_op jit(solution)/shard_map/psum | solution.py:23
  94.2 0.0 copy-start
  94.2 2.7 divide_convert_fusion
  96.9 0.0 all-gather.3.cloned.1.call-update
  96.9 0.0 all-gather.5.cloned.1.call-start
  97.0 0.7 all-gather.5.cloned.1.call-update
  97.7 0.0 copy-done
  97.7 0.1 broadcast_bitcast_fusion
  97.8 34.0 %all-gather.3.cloned.1.call-done = bf16[256,8192]{1,0:T(8,128)(2,1)} async-done(((bf16[256,2048]{1,0:T(8,128)(2,1)}), bf16[256,8192]{1,0:T(8,128)(2,1)}) %all-gather.3.cloned.1.call-update) | async-done | bytes 4194320 | tf_op jit(solution)/shard_map/all_gather | solution.py:25
  131.7 365.9 %all-gather.5.cloned.1.call-done = bf16[8192,2048]{1,0:T(8,128)(2,1)} async-done(((bf16[256,2048]{1,0:T(8,128)(2,1)}), bf16[8192,2048]{1,0:T(8,128)(2,1)}) %all-gather.5.cloned.1.call-update) | async-done | bytes 33554448 | tf_op jit(solution)/shard_map/all_gather | solution.py:26
  497.6 16.3 %fusion.4 = (f32[2048]{0:T(1024)S(1)}, f32[256,2048]{1,0:T(8,128)S(1)}) fusion(f32[2048]{0:T(1024)S(1)} %bitcast.14, bf16[256,8192]{1,0:T(8,128)(2,1)} %all-gather.3.cloned.1.call-done, bf16[8192,2048]{1,0:T(8,128)(2,1)} %all-gather.5.cloned.1.call-done), kind=kOutput, calls=%fused_computation.15 | convolution fusion | flops 8591505408 | bytes 39862272 | tf_op jit(solution)/shard_map/dot_general | solution.py:27
  513.9 78.7 %psum.15 = f32[2048]{0:T(1024)S(1)} all-reduce(f32[2048]{0:T(1024)S(1)} %get-tuple-element.5), channel_id=1, replica_groups=mesh['row'=32,'col'=4] {'row'}, use_global_device_ids=true, to_apply=%region_3.0 | all-reduce | flops 2048 | bytes 16384 | tf_op jit(solution)/shard_map/psum | solution.py:35
  592.6 1.6 broadcast_multiply_fusion
  (6 shorter events, 0.0 us)
Async XLA Ops:
  6.5 125.2 %all-gather.3.cloned.1.call-start = ((), (), s32[]{:S(2)}) async-start(), calls=%async_computation | async-start | bytes 5242880 | tf_op jit(solution)/shard_map/all_gather | solution.py:25
  94.2 3.5 copy-start
  96.9 400.7 %all-gather.5.cloned.1.call-start = ((), (), s32[]{:S(2)}) async-start(), calls=%async_computation.1 | async-start | bytes 34603008 | tf_op jit(solution)/shard_map/all_gather | solution.py:26
Sparse Core Ops, SparseCore 0:
  97.0 34.6 all-gather.2
  133.4 364.2 all-gather.4
where the time goes:
time: 601 us
  waiting for transfers between devices  401 us (67%)
  blocking collectives  164 us (27%)
  matrix products  16.3 us (3%)
  between operations  13.5 us (2%)
  other arithmetic  6.62 us (1%)
    all_gather x1, waiting for transfers between devices, body(): right = lax.all_gather(stochastic, 'row', axis=0, tiled=True)  366 us
    psum x1, blocking collectives, body(): mass = lax.psum(jnp.sum(base, axis=0), 'row')  85.2 us
    psum x1, blocking collectives, body(): totals = lax.psum(partial_totals, 'row')  78.7 us
    all_gather x1, waiting for transfers between devices, body(): left = lax.all_gather(stochastic, 'col', axis=1, tiled=True)  34 us
    dot_general x1, matrix products, body(): expanded = jnp.dot(left, right, preferred_element_type=jnp.float32)  16.3 us
  transfers between devices with their start and end apart: 2, of which 2 were waited for; matrix products, arithmetic and copies ran while one was open for 0% of the time, Pallas kernels for 0%

commit v1 on v0

v1 whole, which is shorter than its diff:
```python
import jax
import jax.numpy as jnp
from jax import lax
from jax.experimental import pallas as pl
from jax.experimental.pallas import tpu as pltpu
from jax.sharding import PartitionSpec as P

MESH = pl.DeviceIdType.MESH
F32 = jnp.float32
BF16 = jnp.bfloat16


class Place:
    def __init__(self):
        row, col = lax.axis_index("row"), lax.axis_index("col")
        self.row, self.col = row, col
        self.yl, self.z, self.x = row // 16, (row // 4) % 4, row % 4
        self.yh, self.c = col // 2, col % 2

    def dev(self, x=None, z=None, yl=None, yh=None, c=None):
        x = self.x if x is None else x
        z = self.z if z is None else z
        yl = self.yl if yl is None else yl
        yh = self.yh if yh is None else yh
        c = self.c if c is None else c
        return (yl * 16 + z * 4 + x, yh * 2 + c)


class Copies:
    def __init__(self, send_sem, recv_sem, me):
        self.send_sem, self.recv_sem, self.me = send_sem, recv_sem, me
        self.ids, self.sent = {}, []

    def slot(self, name):
        return self.ids.setdefault(name, len(self.ids))

    def make(self, name, src, dst, dev):
        k = self.slot(name)
        return pltpu.make_async_remote_copy(
            src_ref=src, dst_ref=dst, send_sem=self.send_sem.at[k], recv_sem=self.recv_sem.at[k],
            device_id=dev, device_id_type=MESH)

    def send(self, name, src, dst, dev):
        copy = self.make(name, src, dst, dev)
        copy.start()
        self.sent.append(copy)

    def wait(self, name, landed, dev):
        self.make(name, landed, landed, dev).wait_recv()

    def drain(self):
        for copy in self.sent:
            copy.wait_send()


def greet(devices):
    barrier = pltpu.get_barrier_semaphore()
    for dev in devices:
        pl.semaphore_signal(barrier, inc=1, device_id=dev, device_id_type=MESH)
    pl.semaphore_wait(barrier, len(devices))


def normalise_kernel(tile, flow, pattern, keep, s_out, km_out, xs, zs, kx, km, send_sem, recv_sem, local_sem):
    me = Place()
    rows, cols = flow.shape
    nt = cols // tile
    wide = cols // 4
    others = [(dz, dy) for dy in (0, 1) for dz in range(4) if (dz, dy) != (0, 0)]
    net = Copies(send_sem, recv_sem, me)
    greet([me.dev(x=(me.x + d) % 4) for d in (1, 2, 3)]
          + [me.dev(z=(me.z + dz) % 4, yl=(me.yl + dy) % 2) for dz, dy in others])

    def base(t):
        on = (pattern[0, t] > 0).astype(F32)
        block = flow[:, t * tile:(t + 1) * tile].astype(F32) * on
        r = lax.broadcasted_iota(jnp.int32, (rows, tile), 0) + me.row * rows
        k = lax.broadcasted_iota(jnp.int32, (rows, tile), 1) + (me.col * cols + t * tile)
        return block + (r == k).astype(F32)

    for t in range(nt):
        xs[me.x, :, t * tile:(t + 1) * tile] = jnp.sum(base(t), axis=0, keepdims=True)
    for d in (1, 3, 2):
        net.send(("x", d), xs.at[me.x], xs.at[me.x], me.dev(x=(me.x + d) % 4))
    for t in range(nt):
        kept = jnp.logical_or(keep[0, t] > 0, me.row == me.col * nt + t).astype(F32)
        kx[:, t * tile:(t + 1) * tile] = jnp.broadcast_to(kept, (8, tile))
    chunk = lambda j: kx.at[:, pl.ds(pl.multiple_of(j * wide, wide), wide)]
    for d in (1, 3, 2):
        to = (me.z + d) % 4
        net.send(("k", d), chunk(to), km.at[me.z], me.dev(z=to))
    own = pltpu.make_async_copy(chunk(me.z), km.at[me.z], local_sem)
    own.start()
    for d in (1, 3, 2):
        src = (me.x - d + 4) % 4
        net.wait(("x", d), xs.at[src], me.dev(x=src))
    here = me.yl * 4 + me.z
    zs[here] = xs[0] + xs[1] + xs[2] + xs[3]
    for dz, dy in others:
        net.send(("z", dz, dy), zs.at[here], zs.at[here], me.dev(z=(me.z + dz) % 4, yl=(me.yl + dy) % 2))
    for dz, dy in others:
        z, yl = (me.z - dz + 4) % 4, (me.yl + dy) % 2
        net.wait(("z", dz, dy), zs.at[yl * 4 + z], me.dev(z=z, yl=yl))
    mass = ((zs[0] + zs[1]) + (zs[2] + zs[3])) + ((zs[4] + zs[5]) + (zs[6] + zs[7]))
    inverse = 1.0 / mass
    for t in range(nt):
        s_out[:, t * tile:(t + 1) * tile] = (base(t) * inverse[:, t * tile:(t + 1) * tile]).astype(BF16)
    own.wait()
    for d in (1, 3, 2):
        src = (me.z - d + 4) % 4
        net.wait(("k", d), km.at[src], me.dev(z=src))
    km_out[...] = km[...]
    net.drain()


def product_kernel(s, km, out, scale_out, a, b, relay, c, ts, sc, send_sem, recv_sem, local_sem):
    me = Place()
    rows, cols = s.shape
    half = rows // 2
    wide = cols // 4
    x, z, yl, yh, core = me.x, me.z, me.yl, me.yh, me.c
    y = yh * 2 + yl
    net = Copies(send_sem, recv_sem, me)
    zp, zm, z2 = (z + 1) % 4, (z + 3) % 4, (z + 2) % 4
    xp, xm, x2 = (x + 1) % 4, (x + 3) % 4, (x + 2) % 4
    turn = 1 + 2 * core
    yn, ys = (y + turn) % 4, (y + 4 - turn) % 4
    group = [(dx, dy) for dy in (0, 1) for dx in range(4) if (dx, dy) != (0, 0)]
    mate = me.dev(c=1 - core)
    to_y = me.dev(yl=yn % 2, yh=yn // 2)
    from_y = me.dev(yl=ys % 2, yh=ys // 2)
    greet([me.dev(z=zp), me.dev(z=zm), me.dev(z=z2), to_y, from_y, mate]
          + [me.dev(x=(x + dx) % 4, yl=(yl + dy) % 2) for dx, dy in group])

    q0, q1 = yh * 2 + core, (1 - yh) * 2 + core
    q_of = (q0, q1)

    def a_at(q, zz, h=None):
        if h is None:
            return a.at[q, pl.ds(pl.multiple_of(zz * rows, rows), rows)]
        return a.at[q, pl.ds(pl.multiple_of(zz * rows + h * half, half), half)]

    def b_at(yy, zz, xx, h=None):
        start = (yy * 16 + zz * 4 + xx) * rows
        if h is None:
            return b.at[pl.ds(pl.multiple_of(start, rows), rows)]
        return b.at[pl.ds(pl.multiple_of(start + h * half, half), half)]

    def s_chunk(j):
        return s.at[:, pl.ds(pl.multiple_of(j * wide, wide), wide)]

    def s_half(h):
        return s.at[pl.ds(h * half, half)]

    z_order = (z, zp, zm, z2)
    pieces = [(yl, zz) for zz in z_order] + [(1 - yl, zz) for zz in z_order]

    def spread_x(i, src):
        yy, zz = pieces[i]
        net.send(("bx+", i), src, b_at(yy, zz, x), me.dev(x=xp))
        net.send(("bx-", i), src, b_at(yy, zz, x), me.dev(x=xm))

    def forward_x(i):
        yy, zz = pieces[i]
        net.wait(("bx+", i), b_at(yy, zz, xm), me.dev(x=xm))
        net.send(("bf+", i), b_at(yy, zz, xm, 0), b_at(yy, zz, xm, 0), me.dev(x=xp))
        net.wait(("bx-", i), b_at(yy, zz, xp), me.dev(x=xp))
        net.send(("bf-", i), b_at(yy, zz, xp, 1), b_at(yy, zz, xp, 1), me.dev(x=xm))

    def last_x(i):
        yy, zz = pieces[i]
        net.wait(("bf+", i), b_at(yy, zz, x2, 0), me.dev(x=xm))
        net.wait(("bf-", i), b_at(yy, zz, x2, 1), me.dev(x=xp))

    def cross_y(i, src):
        yy, zz = pieces[i]
        net.send(("by", i), src, b_at(yy, zz, x), me.dev(yl=1 - yl))

    def home(i):
        yy, zz = pieces[i]
        if i < 4:
            name, src = {1: ("bz-", zp), 2: ("bz+", zm), 3: ("bz2", z2)}[i]
            net.wait(name, b_at(yl, zz, x), me.dev(z=src))
            spread_x(i, b_at(yl, zz, x))
            cross_y(i, b_at(yl, zz, x))
        else:
            net.wait(("by", i - 4), b_at(yy, zz, x), me.dev(yl=1 - yl))
            spread_x(i, b_at(yy, zz, x))

    def to_mate(p, k, h, src):
        zz = (z, zm, zp, z2)[k]
        net.send(("ac", p, k, h), src, a_at(q_of[p], zz, h), mate)

    def z_ring(p, src):
        for first in (0, 1):
            h = first
            net.send(("az+", p, h), src(h), a_at(q_of[p], z, h), me.dev(z=zp))
            h = 1 - first
            net.send(("az-", p, h), src(h), a_at(q_of[p], z, h), me.dev(z=zm))

    def z_take(p, k, h):
        q = q_of[p]
        if k == 1:
            net.wait(("az+", p, h), a_at(q, zm, h), me.dev(z=zm))
            if h == 0:
                net.send(("af+", p), a_at(q, zm, 0), a_at(q, zm, 0), me.dev(z=zp))
            to_mate(p, 1, h, a_at(q, zm, h))
        elif k == 2:
            net.wait(("az-", p, h), a_at(q, zp, h), me.dev(z=zp))
            if h == 1:
                net.send(("af-", p), a_at(q, zp, 1), a_at(q, zp, 1), me.dev(z=zm))
            to_mate(p, 2, h, a_at(q, zp, h))
        else:
            net.wait(("af+", p) if h == 0 else ("af-", p), a_at(q, z2, h), me.dev(z=zm if h == 0 else zp))
            to_mate(p, 3, h, a_at(q, z2, h))

    net.send("bz+", s_chunk(zp), b_at(yl, z, x), me.dev(z=zp))
    net.send("bz-", s_chunk(zm), b_at(yl, z, x), me.dev(z=zm))
    net.send("bz2", s_chunk(z2), b_at(yl, z, x), me.dev(z=z2))
    spread_x(0, s_chunk(z))
    cross_y(0, s_chunk(z))
    z_ring(0, s_half)
    for h in (0, 1):
        net.send(("ay1", h), s_half(h), relay.at[pl.ds(h * half, half)], to_y)
    for h in (0, 1):
        to_mate(0, 0, h, s_half(h))
    local = [pltpu.make_async_copy(s_chunk(z), b_at(yl, z, x), local_sem.at[0]),
             pltpu.make_async_copy(s, a_at(q0, z), local_sem.at[1])]
    for copy in local:
        copy.start()

    def relay_y(h):
        part = relay.at[pl.ds(h * half, half)]
        net.wait(("ay1", h), part, from_y)
        net.send(("ay2", h), part, a_at((ys // 2) * 2 + core, z, h), to_y)

    def take_y(h):
        net.wait(("ay2", h), a_at(q1, z, h), from_y)
        src = lambda k: a_at(q1, z, k)
        net.send(("az+", 1, h), src(h), src(h), me.dev(z=zp))
        net.send(("az-", 1, h), src(h), src(h), me.dev(z=zm))
        to_mate(1, 0, h, src(h))

    home(1)
    home(2)
    forward_x(0)
    relay_y(0)
    home(3)
    forward_x(1)
    home(4)
    z_take(0, 1, 0)
    z_take(0, 2, 1)
    relay_y(1)
    forward_x(2)
    home(5)
    z_take(0, 1, 1)
    z_take(0, 2, 0)
    take_y(0)
    forward_x(3)
    home(6)
    take_y(1)
    z_take(0, 3, 0)
    z_take(0, 3, 1)
    forward_x(4)
    home(7)
    z_take(1, 1, 0)
    z_take(1, 2, 0)
    forward_x(5)
    forward_x(6)
    z_take(1, 1, 1)
    z_take(1, 2, 1)
    forward_x(7)
    for i in range(8):
        last_x(i)
    for copy in local:
        copy.wait()

    def mate_ready(p):
        q = (yh if p == 0 else 1 - yh) * 2 + 1 - core
        for k, zz in enumerate((z, zm, zp, z2)):
            for h in (0, 1):
                net.wait(("ac", p, k, h), a_at(q, zz, h), mate)

    def part(q, zz, n):
        left = a[q, pl.ds(pl.multiple_of(zz * rows, rows), rows)]
        right = b[pl.ds(pl.multiple_of(q * cols, cols), cols), pl.ds(pl.multiple_of(n * 256, 256), 256)]
        return jnp.dot(left, right, preferred_element_type=F32)

    def early(step, _):
        zz, n = step // 2, step % 2
        at = pl.ds(pl.multiple_of(n * 256, 256), 256)
        c[zz, :, at] = part(yh * 2, zz, n) + part(yh * 2 + 1, zz, n)
        return _

    mate_ready(0)
    lax.fori_loop(0, 8, early, 0)
    z_take(1, 3, 0)
    z_take(1, 3, 1)
    mate_ready(1)
    ts[yl * 4 + x] = jnp.zeros(ts.shape[1:], F32)
    for k, (zz, d) in enumerate(((z2, 2), (zp, 1), (zm, 3), (z, 0))):
        def late(n, _, zz=zz):
            at = pl.ds(pl.multiple_of(n * 256, 256), 256)
            full = c[zz, :, at] + part((1 - yh) * 2, zz, n) + part((1 - yh) * 2 + 1, zz, n)
            full = full * km[zz, 0:1, at]
            full = full * full
            c[zz, :, at] = full
            ts[yl * 4 + x, :, at] += jnp.sum(full, axis=0, keepdims=True)
            return _

        lax.fori_loop(0, 2, late, 0)
        mine = out.at[:, pl.ds(pl.multiple_of(z * wide, wide), wide)]
        if d:
            net.send(("c", d), c.at[zz], mine, me.dev(z=(z + d) % 4))
        else:
            keep = pltpu.make_async_copy(c.at[zz], mine, local_sem.at[2])
            keep.start()
    for dx, dy in group:
        net.send(("t", dx, dy), ts.at[yl * 4 + x], ts.at[yl * 4 + x], me.dev(x=(x + dx) % 4, yl=(yl + dy) % 2))
    for dx, dy in group:
        xx, yy = (x - dx + 4) % 4, (yl + dy) % 2
        net.wait(("t", dx, dy), ts.at[yy * 4 + xx], me.dev(x=xx, yl=yy))
    total = ((ts[0] + ts[1]) + (ts[2] + ts[3])) + ((ts[4] + ts[5]) + (ts[6] + ts[7]))
    sc[z] = (rows * 32) / total
    for d in (1, 3, 2):
        net.send(("s", d), sc.at[z], sc.at[z], me.dev(z=(z + d) % 4))
    keep.wait()
    for d in (1, 3, 2):
        src = (z - d + 4) % 4
        net.wait(("s", d), sc.at[src], me.dev(z=src))
    scale_out[...] = sc[...]
    for d in (1, 3, 2):
        src = (z - d + 4) % 4
        net.wait(("c", d), out.at[:, pl.ds(pl.multiple_of(src * wide, wide), wide)], me.dev(z=src))
    net.drain()


def body(flow, pattern, keep):
    rows, cols = flow.shape
    nt = pattern.shape[1]
    tile = cols // nt
    wide = cols // 4
    vmem = pl.BlockSpec(memory_space=pltpu.VMEM)
    smem = pl.BlockSpec(memory_space=pltpu.SMEM)
    anyspace = pl.BlockSpec(memory_space=pl.ANY)
    s, km = pl.pallas_call(
        lambda *refs: normalise_kernel(tile, *refs),
        out_shape=(jax.ShapeDtypeStruct((rows, cols), BF16), jax.ShapeDtypeStruct((4, 8, wide), F32)),
        in_specs=[vmem, smem, smem],
        out_specs=(vmem, vmem),
        scratch_shapes=[
            pltpu.VMEM((4, 1, cols), F32),
            pltpu.VMEM((8, 1, cols), F32),
            pltpu.VMEM((8, cols), F32),
            pltpu.VMEM((4, 8, wide), F32),
            pltpu.SemaphoreType.DMA((13,)),
            pltpu.SemaphoreType.DMA((13,)),
            pltpu.SemaphoreType.DMA,
        ],
        compiler_params=pltpu.CompilerParams(collective_id=0, has_side_effects=True),
        name="normalise",
    )(flow, pattern, keep)
    messages = 92
    inflated, scale = pl.pallas_call(
        product_kernel,
        out_shape=(jax.ShapeDtypeStruct((rows, cols), F32), jax.ShapeDtypeStruct((4, 1, wide), F32)),
        in_specs=[anyspace, vmem],
        out_specs=(anyspace, vmem),
        scratch_shapes=[
            pltpu.VMEM((4, 4 * rows, cols), BF16),
            pltpu.VMEM((32 * rows, wide), BF16),
            pltpu.VMEM((rows, cols), BF16),
            pltpu.VMEM((4, rows, wide), F32),
            pltpu.VMEM((8, 1, wide), F32),
            pltpu.VMEM((4, 1, wide), F32),
            pltpu.SemaphoreType.DMA((messages,)),
            pltpu.SemaphoreType.DMA((messages,)),
            pltpu.SemaphoreType.DMA((3,)),
        ],
        compiler_params=pltpu.CompilerParams(
            collective_id=1, has_side_effects=True, vmem_limit_bytes=48 * 1024 * 1024),
        name="product",
    )(s, km)
    return inflated * scale.reshape(1, cols)


def solution(mesh):
    return jax.shard_map(
        body,
        mesh=mesh,
        in_specs=(P("row", "col"), P("row", "col"), P("row", "col")),
        out_specs=P("row", "col"),
        check_vma=False,
    )
```

time: 601 us -> 133 us (0.22)
  waiting for transfers between devices: 401 us -> 0 us
  blocking collectives: 164 us -> 0 us
  Pallas kernels: 0 us -> 129 us
  matrix products: 16.3 us -> 0 us
  between operations: 13.5 us -> 0.03 us
    all_gather x2 -> x0, waiting for transfers between devices: 400 us -> none  [the longest x1 366 us: body(): right = lax.all_gather(stochastic, 'row', axis=0, tiled=True)]
    psum x2 -> x0, blocking collectives: 164 us -> none  [the longest x1 85.2 us: body(): mass = lax.psum(jnp.sum(base, axis=0), 'row')]
    pallas_call x0 -> x2, Pallas kernels: none -> 129 us  [the longest x1 112 us: body(): pl.pallas_call(product_kernel, out_shape=(jax.ShapeDtypeStruct((rows, col...]
    dot_general x1 -> x0, matrix products: 16.3 us -> none  [body(): expanded = jnp.dot(left, right, preferred_element_type=jnp.float32)]
  transfers between devices with their start and end apart: 2 -> 0, of which waited for: 2 -> 0; matrix products, arithmetic and copies ran while one was open for 0% -> 0% of each run, Pallas kernels for 0% -> 0%
where the time goes in v1:
time: 133 us; the launch traced here: 132 us
  Pallas kernels  129 us (97%)
  local copies, waits for them, and re-layouts  2.06 us (2%)
  other arithmetic  1.62 us (1%)
    pallas_call x1, Pallas kernels, body(): pl.pallas_call(product_kernel, out_shape=(jax.ShapeDtypeStruct((rows, col...  112 us
    pallas_call x1, Pallas kernels, body(): pl.pallas_call(lambda *refs: normalise_kernel(tile, *refs), out_shape=(ja...  16.7 us

profile of v1, /device:TPU:0, one launch (start us, length us, event | category | flops | bytes accessed | tf_op | source)
XLA Modules:
  0.0 132.2 jit_solution(9129145544078927292)
XLA Ops:
  0.0 16.7 %normalise.1 = (bf16[256,2048]{1,0:T(8,128)(2,1)}, f32[4,8,512]{2,1,0:T(8,128)}) custom-call(bf16[256,2048]{1,0:T(8,128)(2,1)} %refs_0_.1, s32[1,8]{1,0:T(1,128)} %refs_1_.1, s32[1,8]{1,0:T(1,128)} %refs_2_.1), custom_call_target="tpu_custom_call" | custom-call | tf_op jit(solution)/shard_map/normalise/pallas_call | solution.py:345
  16.7 0.0 copy-start
  16.7 1.2 copy-done
  17.9 0.0 copy-start.1
  17.9 0.8 copy-done.1
  18.8 111.8 %product.1 = (f32[256,2048]{1,0:T(8,128)S(1)}, f32[4,1,512]{2,1,0:T(1,128)S(1)}) custom-call(bf16[256,2048]{1,0:T(8,128)(2,1)S(1)} %copy-done, f32[4,8,512]{2,1,0:T(8,128)S(1)} %copy-done.1), custom_call_target="tpu_custom_call" | custom-call | tf_op jit(solution)/shard_map/product/pallas_call | solution.py:363
  130.6 1.6 %broadcast_multiply_fusion = f32[256,2048]{1,0:T(8,128)} fusion(f32[256,2048]{1,0:T(8,128)S(1)} %get-tuple-element.11, f32[2048]{0:T(1024)S(1)} %bitcast.1), kind=kLoop, calls=%fused_computation | loop fusion | flops 524288 | bytes 4202496 | tf_op jit(solution)/shard_map/mul | solution.py:383
Async XLA Ops:
  16.7 1.2 copy-start
  17.9 0.8 copy-start.1

commit v2 on v0

v2 whole, which is shorter than its diff:
```python
import jax
import jax.numpy as jnp
from jax import lax
from jax.experimental import pallas as pl
from jax.experimental.pallas import tpu as pltpu
from jax.sharding import PartitionSpec as P

MESH = pl.DeviceIdType.MESH
F32 = jnp.float32
BF16 = jnp.bfloat16


class Place:
    def __init__(self):
        row, col = lax.axis_index("row"), lax.axis_index("col")
        self.row, self.col = row, col
        self.yl, self.z, self.x = row // 16, (row // 4) % 4, row % 4
        self.yh, self.c = col // 2, col % 2

    def dev(self, x=None, z=None, yl=None, yh=None, c=None):
        x = self.x if x is None else x
        z = self.z if z is None else z
        yl = self.yl if yl is None else yl
        yh = self.yh if yh is None else yh
        c = self.c if c is None else c
        return (yl * 16 + z * 4 + x, yh * 2 + c)


class Copies:
    def __init__(self, send_sem, recv_sem, me):
        self.send_sem, self.recv_sem, self.me = send_sem, recv_sem, me
        self.ids, self.sent = {}, []

    def slot(self, name):
        return self.ids.setdefault(name, len(self.ids))

    def make(self, name, src, dst, dev):
        k = self.slot(name)
        return pltpu.make_async_remote_copy(
            src_ref=src, dst_ref=dst, send_sem=self.send_sem.at[k], recv_sem=self.recv_sem.at[k],
            device_id=dev, device_id_type=MESH)

    def send(self, name, src, dst, dev):
        copy = self.make(name, src, dst, dev)
        copy.start()
        self.sent.append(copy)

    def wait(self, name, landed, dev):
        self.make(name, landed, landed, dev).wait_recv()

    def drain(self):
        for copy in self.sent:
            copy.wait_send()


def kernel(tile, flow, pattern, keep, q_out, gs_out, a, b, m, araw, braw, xraw, c, cq, xs, zs, inv, kx, km, ts, gsend, gs,
           send_sem, recv_sem, local_sem):
    me = Place()
    rows, cols = flow.shape
    nt = cols // tile
    half = rows // 2
    wide = cols // 4
    ring = 3 * rows // 4
    parts = ((0, ring // 2), (ring // 2, ring // 2), (ring, rows - ring))
    x, z, yl, yh, core = me.x, me.z, me.yl, me.yh, me.c
    net = Copies(send_sem, recv_sem, me)
    zp, zm, z2 = (z + 1) % 4, (z + 3) % 4, (z + 2) % 4
    xp, xm, x2 = (x + 1) % 4, (x + 3) % 4, (x + 2) % 4
    around = [(d, dy) for dy in (0, 1) for d in range(4) if (d, dy) != (0, 0)]
    mate, across, beside = me.dev(c=1 - core), me.dev(yh=1 - yh), me.dev(yl=1 - yl)
    barrier = pltpu.get_barrier_semaphore()
    peers = ([me.dev(x=(x + d) % 4, yl=(yl + dy) % 2) for d, dy in around]
             + [me.dev(z=(z + d) % 4, yl=(yl + dy) % 2) for d, dy in around if d] + [mate, across])
    for dev in peers:
        pl.semaphore_signal(barrier, inc=1, device_id=dev, device_id_type=MESH)

    q0, q1 = yh * 2 + core, (1 - yh) * 2 + core
    q_of = (q0, q1)

    def block(yy, zz, xx):
        return yy * 16 + zz * 4 + xx

    def a_at(q, zz, start=0, size=rows):
        return a.at[q, pl.ds(pl.multiple_of(zz * rows + start, 32), size)]

    def b_at(yy, zz, xx, start=0, size=rows):
        return b.at[pl.ds(pl.multiple_of(block(yy, zz, xx) * rows + start, half), size)]

    def chunk(ref, j):
        return ref.at[:, pl.ds(pl.multiple_of(j * wide, wide), wide)]

    def eye(first_row, first_col):
        r = lax.broadcasted_iota(jnp.int32, (rows, tile), 0)
        k = lax.broadcasted_iota(jnp.int32, (rows, tile), 1)
        return (r - k == first_col - first_row).astype(F32)

    for t in range(nt):
        at = slice(t * tile, (t + 1) * tile)
        on = (pattern[0, t] > 0).astype(F32)
        masked = flow[:, at].astype(F32) * on
        m[:, at] = masked.astype(BF16)
        masked = masked + eye(me.row * rows, me.col * cols + t * tile)
        xs[x, :, at] = jnp.sum(masked, axis=0, keepdims=True)
        kept = jnp.logical_or(keep[0, t] > 0, me.row == me.col * nt + t).astype(F32)
        kx[:, at] = jnp.broadcast_to(kept, (8, tile))
    km[z] = kx[:, pl.ds(pl.multiple_of(z * wide, wide), wide)]
    pl.semaphore_wait(barrier, len(peers))

    for d in (1, 3, 2):
        net.send(("mx", d), xs.at[x], xs.at[x], me.dev(x=(x + d) % 4))
    net.send("bz+", chunk(m, zp), braw.at[0], me.dev(z=zp))
    net.send("bz-", chunk(m, zm), braw.at[1], me.dev(z=zm))
    net.send(("bx+", 0), chunk(m, z), xraw.at[0], me.dev(x=xp))
    net.send(("bx-", 0), chunk(m, z), xraw.at[1], me.dev(x=xm))
    for d in (1, 3, 2):
        src = (x - d + 4) % 4
        net.wait(("mx", d), xs.at[src], me.dev(x=src))
    here = yl * 4 + z
    zs[here] = (xs[0] + xs[1]) + (xs[2] + xs[3])
    for d, dy in around:
        net.send(("mz", d, dy), zs.at[here], zs.at[here], me.dev(z=(z + d) % 4, yl=(yl + dy) % 2))
    net.send("bz2", chunk(m, z2), braw.at[2], me.dev(z=z2))
    for d in (1, 3, 2):
        net.send(("k", d), chunk(kx, (z + d) % 4), km.at[z], me.dev(z=(z + d) % 4))
    for first in (0, 1):
        for name, h, k, to in (("az0+", first, 0, zp), ("az0-", 1 - first, 1, zm)):
            at = pl.ds(h * half, half)
            net.send((name, h), m.at[at], araw.at[k, at], me.dev(z=to))

    z_order = (z, zp, zm, z2)
    pieces = [(yl, zz) for zz in z_order] + [(1 - yl, zz) for zz in z_order]

    def landed_x(i, k, start=0, size=rows):
        if i == 0:
            return xraw.at[k, pl.ds(start, size)]
        yy, zz = pieces[i]
        return b_at(yy, zz, (xm, xp, x2)[k], start, size)

    def sent_x(i, k, start=0, size=rows):
        if i == 0:
            return xraw.at[k, pl.ds(start, size)]
        yy, zz = pieces[i]
        return b_at(yy, zz, x if k < 2 else (xm if start == 0 else xp), start, size)

    def spread_x(i, src):
        net.send(("bx+", i), src, sent_x(i, 0), me.dev(x=xp))
        net.send(("bx-", i), src, sent_x(i, 1), me.dev(x=xm))

    def forward_x(i):
        net.wait(("bx+", i), landed_x(i, 0), me.dev(x=xm))
        net.send(("bf+", i), landed_x(i, 0, 0, half), sent_x(i, 2, 0, half), me.dev(x=xp))
        net.wait(("bx-", i), landed_x(i, 1), me.dev(x=xp))
        net.send(("bf-", i), landed_x(i, 1, half, half), sent_x(i, 2, half, half), me.dev(x=xm))

    def last_x(i):
        net.wait(("bf+", i), landed_x(i, 2, 0, half), me.dev(x=xm))
        net.wait(("bf-", i), landed_x(i, 2, half, half), me.dev(x=xp))

    forward_x(0)

    for d, dy in around:
        zz, yy = (z - d + 4) % 4, (yl + dy) % 2
        net.wait(("mz", d, dy), zs.at[yy * 4 + zz], me.dev(z=zz, yl=yy))
    mass = ((zs[0] + zs[1]) + (zs[2] + zs[3])) + ((zs[4] + zs[5]) + (zs[6] + zs[7]))
    inv[...] = 1.0 / mass

    def normalise(dst, src, count, first_row, first_tile):
        def step(t, _):
            at = pl.ds(pl.multiple_of(t * tile, tile), tile)
            there = pl.ds(pl.multiple_of((first_tile + t) * tile, tile), tile)
            value = src[:, at].astype(F32) + eye(first_row, me.col * cols + (first_tile + t) * tile)
            dst[:, at] = (value * inv[:, there]).astype(BF16)
            return _

        lax.fori_loop(0, count, step, 0)

    def normalise_b(dst_x, zz, src):
        normalise(b_at(yl, zz, dst_x), src, wide // tile, block(yl, zz, dst_x) * rows, z * (wide // tile))

    def normalise_a(zz, src):
        normalise(a_at(q0, zz), src, nt, block(yl, zz, x) * rows, 0)

    def home(i):
        yy, zz = pieces[i]
        piece = b_at(yy, zz, x)
        if i < 4:
            name, k, src = {1: ("bz-", 1, zp), 2: ("bz+", 0, zm), 3: ("bz2", 2, z2)}[i]
            net.wait(name, braw.at[k], me.dev(z=src))
            normalise_b(x, zz, braw.at[k])
            spread_x(i, piece)
            net.send(("by", i), piece, piece, beside)
        else:
            net.wait(("by", i - 4), piece, beside)
            spread_x(i, piece)

    def take_z0(k, h):
        at = pl.ds(h * half, half)
        if k == 0:
            net.wait(("az0+", h), araw.at[0, at], me.dev(z=zm))
            if h == 0:
                net.send("af0+", araw.at[0, at], araw.at[2, at], me.dev(z=zp))
        elif k == 1:
            net.wait(("az0-", h), araw.at[1, at], me.dev(z=zp))
            if h == 1:
                net.send("af0-", araw.at[1, at], araw.at[2, at], me.dev(z=zm))
        elif h == 0:
            net.wait("af0+", araw.at[2, at], me.dev(z=zm))
        else:
            net.wait("af0-", araw.at[2, at], me.dev(z=zp))

    def finish_z0(k):
        zz = (zm, zp, z2)[k]
        normalise_a(zz, araw.at[k])
        net.send(("ac0", k + 1), a_at(q0, zz), a_at(q0, zz), mate)
        start, size = parts[2]
        net.send(("ar", k), a_at(q0, zz, start, size), a_at(q0, zz, start, size), across)

    def to_mate(k, p):
        zz = (z, zm, zp, z2)[k]
        net.send(("ac1", k, p), a_at(q1, zz, *parts[p]), a_at(q1, zz, *parts[p]), mate)

    def take_y(p):
        at = a_at(q1, z, *parts[p])
        net.wait(("ay", p), at, across)
        if p < 2:
            net.send(("az1+", p), at, at, me.dev(z=zp))
            net.send(("az1-", p), at, at, me.dev(z=zm))
        to_mate(0, p)

    def take_rest(k):
        net.wait(("ar", k), a_at(q1, (zm, zp, z2)[k], *parts[2]), across)
        to_mate(k + 1, 2)

    def take_z1(k, p):
        at = a_at(q1, (zm, zp, z2)[k], *parts[p])
        if k == 0:
            net.wait(("az1+", p), at, me.dev(z=zm))
            if p == 0:
                net.send("af1+", at, at, me.dev(z=zp))
        elif k == 1:
            net.wait(("az1-", p), at, me.dev(z=zp))
            if p == 1:
                net.send("af1-", at, at, me.dev(z=zm))
        elif p == 0:
            net.wait("af1+", at, me.dev(z=zm))
        else:
            net.wait("af1-", at, me.dev(z=zp))
        to_mate(k + 1, p)

    def mate0(k):
        at = a_at(yh * 2 + 1 - core, (z, zm, zp, z2)[k])
        net.wait(("ac0", k), at, mate)

    def mate1(k, ps=(0, 1, 2)):
        for p in ps:
            net.wait(("ac1", k, p), a_at((1 - yh) * 2 + 1 - core, (z, zm, zp, z2)[k], *parts[p]), mate)

    def units(yy, piece, ks, first=False):
        zi = z_order[piece]
        deep = 4 * rows
        left_at = pl.ds(pl.multiple_of((zi % 2) * deep, deep), deep)
        right_at = pl.ds(pl.multiple_of((yy * 4 + zi) * deep, deep), deep)
        q = yy * 2 + zi // 2

        def step(j, _):
            k, n = j // 2, j % 2
            zz = (z + (ks[0] if len(ks) == 1 else k if len(ks) == 4 else ks[0] + 2 * k)) % 4
            at = pl.ds(pl.multiple_of(n * 256, 256), 256)
            left = a[q, pl.ds(pl.multiple_of(zz * rows, rows), rows), left_at]
            value = jnp.dot(left, b[right_at, at], preferred_element_type=F32)
            c[zz, :, at] = value if first else c[zz, :, at] + value
            return _

        lax.fori_loop(0, 2 * len(ks), step, 0)

    home(1)
    normalise_b(x, z, chunk(m, z))
    net.send(("by", 0), b_at(yl, z, x), b_at(yl, z, x), beside)
    home(2)
    normalise_a(z, m)
    for p in (0, 1, 2):
        at = a_at(q0, z, *parts[p])
        net.send(("ay", p), at, at, across)
    net.send(("ac0", 0), a_at(q0, z), a_at(q0, z), mate)
    home(3)
    forward_x(1)
    home(4)
    last_x(0)
    for k, xx in enumerate((xm, xp, x2)):
        normalise_b(xx, z, xraw.at[k])
    take_z0(0, 0)
    take_z0(1, 1)
    forward_x(2)
    home(5)
    take_y(0)
    forward_x(3)
    take_z0(0, 1)
    take_z0(1, 0)
    finish_z0(0)
    finish_z0(1)
    take_y(1)
    take_y(2)
    home(6)
    forward_x(4)
    take_z0(2, 0)
    take_z0(2, 1)
    finish_z0(2)
    home(7)
    forward_x(5)
    for i in (1, 2, 3):
        last_x(i)
    for k in range(4):
        mate0(k)
    mate1(0)
    last_x(4)
    take_rest(0)
    take_rest(1)
    units(yh, 0, (0, 1, 2, 3), first=True)
    forward_x(6)
    last_x(5)
    take_z1(0, 0)
    take_z1(1, 1)
    units(yh, 1, (0, 1, 2, 3))
    units(1 - yh, 0, (0,))
    units(1 - yh, 1, (0,))
    take_rest(2)
    take_z1(0, 1)
    take_z1(1, 0)
    last_x(6)
    units(yh, 2, (0, 1, 2, 3))
    forward_x(7)
    mate1(1)
    mate1(2)
    units(1 - yh, 2, (0,))
    for piece in (0, 1, 2):
        units(1 - yh, piece, (1, 3))
    take_z1(2, 0)
    take_z1(2, 1)
    last_x(7)
    units(yh, 3, (0, 1, 2, 3))
    units(1 - yh, 3, (1, 3))
    mine = yl * 4 + x
    for d in (1, 3, 2):
        src = (z - d + 4) % 4
        net.wait(("k", d), km.at[src], me.dev(z=src))
    ts[mine] = jnp.zeros(ts.shape[1:], F32)

    def finish(d):
        zz = (z + d) % 4
        for n in range(wide // 256):
            at = slice(n * 256, (n + 1) * 256)
            kept = c[zz, :, at] * km[zz, 0:1, at]
            ts[mine, :, at] += jnp.sum(kept * kept, axis=0, keepdims=True)
            top = jnp.max(kept, axis=0, keepdims=True)
            up = jnp.where(top > 0, 32767.0 / jnp.where(top > 0, top, 1.0), 0.0)
            cq[d, :, at] = jnp.round(kept * up).astype(jnp.int32).astype(jnp.int16)
            gsend[d, :, at] = top * (1.0 / 32767.0)
        if d:
            net.send(("c", d), cq.at[d], chunk(q_out, z), me.dev(z=zz))

    finish(1)
    finish(3)
    mate1(3)
    for piece in range(4):
        units(1 - yh, piece, (2,))
    finish(2)
    units(1 - yh, 3, (0,))
    finish(0)
    own = pltpu.make_async_copy(cq.at[0], chunk(q_out, z), local_sem)
    own.start()
    for d, dy in around:
        net.send(("t", d, dy), ts.at[mine], ts.at[mine], me.dev(x=(x + d) % 4, yl=(yl + dy) % 2))
    for d, dy in around:
        xx, yy = (x - d + 4) % 4, (yl + dy) % 2
        net.wait(("t", d, dy), ts.at[yy * 4 + xx], me.dev(x=xx, yl=yy))
    total = ((ts[0] + ts[1]) + (ts[2] + ts[3])) + ((ts[4] + ts[5]) + (ts[6] + ts[7]))
    scale = (rows * 32) / total
    for d in range(4):
        gsend[d, :, wide:] = scale
    gs[z] = gsend[0]
    for d in (1, 3, 2):
        net.send(("s", d), gsend.at[d], gs.at[z], me.dev(z=(z + d) % 4))
    own.wait()
    for d in (1, 3, 2):
        src = (z - d + 4) % 4
        net.wait(("s", d), gs.at[src], me.dev(z=src))
    gs_out[...] = gs[...]
    for d in (1, 3, 2):
        src = (z - d + 4) % 4
        net.wait(("c", d), chunk(q_out, src), me.dev(z=src))
    net.drain()


def body(flow, pattern, keep):
    rows, cols = flow.shape
    tile = cols // pattern.shape[1]
    wide = cols // 4
    vmem = pl.BlockSpec(memory_space=pltpu.VMEM)
    smem = pl.BlockSpec(memory_space=pltpu.SMEM)
    messages = 104
    coded, factors = pl.pallas_call(
        lambda *refs: kernel(tile, *refs),
        out_shape=(jax.ShapeDtypeStruct((rows, cols), jnp.int16), jax.ShapeDtypeStruct((4, 1, 2 * wide), F32)),
        in_specs=[vmem, smem, smem],
        out_specs=(pl.BlockSpec(memory_space=pl.ANY), vmem),
        scratch_shapes=[
            pltpu.VMEM((4, 4 * rows, cols), BF16),
            pltpu.VMEM((32 * rows, wide), BF16),
            pltpu.VMEM((rows, cols), BF16),
            pltpu.VMEM((3, rows, cols), BF16),
            pltpu.VMEM((3, rows, wide), BF16),
            pltpu.VMEM((3, rows, wide), BF16),
            pltpu.VMEM((4, rows, wide), F32),
            pltpu.VMEM((4, rows, wide), jnp.int16),
            pltpu.VMEM((4, 1, cols), F32),
            pltpu.VMEM((8, 1, cols), F32),
            pltpu.VMEM((1, cols), F32),
            pltpu.VMEM((8, cols), F32),
            pltpu.VMEM((4, 8, wide), F32),
            pltpu.VMEM((8, 1, wide), F32),
            pltpu.VMEM((4, 1, 2 * wide), F32),
            pltpu.VMEM((4, 1, 2 * wide), F32),
            pltpu.SemaphoreType.DMA((messages,)),
            pltpu.SemaphoreType.DMA((messages,)),
            pltpu.SemaphoreType.DMA,
        ],
        compiler_params=pltpu.CompilerParams(
            collective_id=0, has_side_effects=True, vmem_limit_bytes=50 * 1024 * 1024),
        name="cluster",
    )(flow, pattern, keep)
    down = factors[:, 0, :wide].reshape(1, cols)
    scale = factors[:, 0, wide:].reshape(1, cols)
    expanded = coded.astype(F32) * down
    return expanded * expanded * scale


def solution(mesh):
    return jax.shard_map(
        body,
        mesh=mesh,
        in_specs=(P("row", "col"), P("row", "col"), P("row", "col")),
        out_specs=P("row", "col"),
        check_vma=False,
    )
```

time: 601 us -> 115 us (0.19)
  waiting for transfers between devices: 401 us -> 0 us
  blocking collectives: 164 us -> 0 us
  Pallas kernels: 0 us -> 110 us
  matrix products: 16.3 us -> 0 us
  between operations: 13.5 us -> 0.02 us
    all_gather x2 -> x0, waiting for transfers between devices: 400 us -> none  [the longest x1 366 us: body(): right = lax.all_gather(stochastic, 'row', axis=0, tiled=True)]
    psum x2 -> x0, blocking collectives: 164 us -> none  [the longest x1 85.2 us: body(): mass = lax.psum(jnp.sum(base, axis=0), 'row')]
    pallas_call x0 -> x1, Pallas kernels: none -> 110 us  [body(): pl.pallas_call(lambda *refs: kernel(tile, *refs), out_shape=(jax.ShapeDty...]
    dot_general x1 -> x0, matrix products: 16.3 us -> none  [body(): expanded = jnp.dot(left, right, preferred_element_type=jnp.float32)]
  transfers between devices with their start and end apart: 2 -> 0, of which waited for: 2 -> 0; matrix products, arithmetic and copies ran while one was open for 0% -> 0% of each run, Pallas kernels for 0% -> 0%
where the time goes in v2:
time: 115 us
  Pallas kernels  110 us (96%)
  local copies, waits for them, and re-layouts  2.54 us (2%)
  other arithmetic  1.83 us (2%)
    pallas_call x1, Pallas kernels, body(): pl.pallas_call(lambda *refs: kernel(tile, *refs), out_shape=(jax.ShapeDty...  110 us
    unnamed x6, local copies, waits for them, and re-layouts  2.53 us

profile of v2, /device:TPU:0, one launch (start us, length us, event | category | flops | bytes accessed | tf_op | source)
XLA Modules:
  0.0 114.6 jit_solution(11250138965352615099)
XLA Ops:
  0.0 0.0 copy-start
  0.0 1.2 %copy-done = bf16[256,2048]{1,0:T(8,128)(2,1)S(1)} copy-done((bf16[256,2048]{1,0:T(8,128)(2,1)S(1)}, bf16[256,2048]{1,0:T(8,128)(2,1)}, u32[]{:S(2)}) %copy-start) | copy-done | bytes 1048600
  1.2 0.0 copy-start.1
  1.2 0.7 copy-done.1
  1.9 0.0 copy-start.2
  1.9 0.7 copy-done.2
  2.5 110.3 %cluster.1 = (s16[256,2048]{1,0:T(8,128)(2,1)S(1)}, f32[4,1,1024]{2,1,0:T(1,128)S(1)}) custom-call(bf16[256,2048]{1,0:T(8,128)(2,1)S(1)} %copy-done, s32[1,8]{1,0:T(1,128)S(1)} %copy-done.1, s32[1,8]{1,0:T(1,128)S(1)} %copy-done.2), custom_call_target="tpu_custom_call" | custom-call | tf_op jit(solution)/shard_map/cluster/pallas_call | solution.py:401
  112.8 1.8 %multiply_multiply_fusion = f32[256,2048]{1,0:T(8,128)} fusion(s16[256,2048]{1,0:T(8,128)(2,1)S(1)} %get-tuple-element.7, f32[2048]{0:T(1024)S(1)} %bitcast.3, f32[2048]{0:T(1024)S(1)} %bitcast.2), kind=kLoop, calls=%fused_computation | loop fusion | flops 2097152 | bytes 3162112 | tf_op jit(solution)/shard_map/mul | solution.py:434
  (1 shorter events, 0.0 us)
Async XLA Ops:
  0.0 1.2 %copy-start = (bf16[256,2048]{1,0:T(8,128)(2,1)S(1)}, bf16[256,2048]{1,0:T(8,128)(2,1)}, u32[]{:S(2)}) copy-start(bf16[256,2048]{1,0:T(8,128)(2,1)} %refs_0_.1) | copy-start | bytes 3145732
  1.2 0.7 copy-start.1
  1.9 0.7 copy-start.2

commit v3 on v2

v3 whole, which is shorter than its diff:
```python
import jax
import jax.numpy as jnp
from jax import lax
from jax.experimental import pallas as pl
from jax.experimental.pallas import tpu as pltpu
from jax.sharding import PartitionSpec as P

MESH = pl.DeviceIdType.MESH
F32 = jnp.float32
BF16 = jnp.bfloat16
RING = 6
ORDER = (
    "start", "mx", ("f", 0), "inv", ("home", 1), ("home", 2), "own", "nb0", "lx0", ("home", 3), ("f", 1), ("home", 4),
    ("f", 2), "z0a", ("f", 3), ("y", 0), ("y", 1), ("y", 2), ("fin", 0), ("f", 4), ("fin", 1), ("home", 5),
    ("home", 6), ("Lz", 0), ("fin", 2), ("home", 7), ("f", 5), ("E", 0), "z1a", ("r", 0), ("f", 6), ("r", 1),
    ("f", 7), "z1b", ("E", 1), ("Lz", 1), ("Lm", 0), ("r", 2), ("Lm", 1), ("E", 2), ("Lz", 2), ("Lm", 2), "z1c",
    ("E", 3), ("Lz", 3), ("Lm", 3), ("C", 1), ("C", 3), ("L2", 0), ("L2", 1), ("L2", 2), ("L2", 3), ("C", 2),
    ("C", 0), "tot",
)


class Place:
    def __init__(self):
        row, col = lax.axis_index("row"), lax.axis_index("col")
        self.row, self.col = row, col
        self.yl, self.z, self.x = row // 16, (row // 4) % 4, row % 4
        self.yh, self.c = col // 2, col % 2

    def dev(self, x=None, z=None, yl=None, yh=None, c=None):
        x = self.x if x is None else x
        z = self.z if z is None else z
        yl = self.yl if yl is None else yl
        yh = self.yh if yh is None else yh
        c = self.c if c is None else c
        return (yl * 16 + z * 4 + x, yh * 2 + c)


class Copies:
    def __init__(self, send_sem, recv_sem, me):
        self.send_sem, self.recv_sem, self.me = send_sem, recv_sem, me
        self.ids, self.sent, self.met = {}, [], set()

    def slot(self, name):
        return self.ids.setdefault(name, len(self.ids))

    def make(self, name, src, dst, dev):
        k = self.slot(name)
        return pltpu.make_async_remote_copy(
            src_ref=src, dst_ref=dst, send_sem=self.send_sem.at[k], recv_sem=self.recv_sem.at[k],
            device_id=dev, device_id_type=MESH)

    def send(self, name, src, dst, dev):
        copy = self.make(name, src, dst, dev)
        copy.start()
        self.sent.append(copy)

    def wait(self, name, landed, dev):
        self.make(name, landed, landed, dev).wait_recv()

    def need(self, name, landed, dev):
        if name not in self.met:
            self.met.add(name)
            self.wait(name, landed, dev)

    def drain(self):
        for copy in self.sent:
            copy.wait_send()


def kernel(tile, flow_hbm, pattern_hbm, keep_hbm, q_out, gs_out, flow, pattern, keep, a, b, m, araw, yraw, braw, xraw, craw, c, cq,
           xs, zs, inv, kx, km, ts, gsend, gs, send_sem, recv_sem, local_sem):
    me = Place()
    rows, cols = flow.shape
    nt = cols // tile
    half = rows // 2
    wide = cols // 4
    ring = RING * rows // 8
    parts = ((0, ring // 2), (ring // 2, ring // 2), (ring, rows - ring))
    x, z, yl, yh, core = me.x, me.z, me.yl, me.yh, me.c
    net = Copies(send_sem, recv_sem, me)
    zp, zm, z2 = (z + 1) % 4, (z + 3) % 4, (z + 2) % 4
    xp, xm, x2 = (x + 1) % 4, (x + 3) % 4, (x + 2) % 4
    around = [(d, dy) for dy in (0, 1) for d in range(4) if (d, dy) != (0, 0)]
    mate, across, beside = me.dev(c=1 - core), me.dev(yh=1 - yh), me.dev(yl=1 - yl)
    fetch = [pltpu.make_async_copy(src, dst, local_sem.at[k])
             for k, (src, dst) in enumerate(((flow_hbm, flow), (pattern_hbm, pattern), (keep_hbm, keep)))]
    for copy in fetch:
        copy.start()
    barrier = pltpu.get_barrier_semaphore()
    peers = ([me.dev(x=(x + d) % 4, yl=(yl + dy) % 2) for d, dy in around]
             + [me.dev(z=(z + d) % 4, yl=(yl + dy) % 2) for d, dy in around if d] + [mate, across])
    for dev in peers:
        pl.semaphore_signal(barrier, inc=1, device_id=dev, device_id_type=MESH)

    q0, q1 = yh * 2 + core, (1 - yh) * 2 + core
    z_mates = (z, zm, zp, z2)
    z_order = (z, zp, zm, z2)
    pieces = [(yl, zz) for zz in z_order] + [(1 - yl, zz) for zz in z_order]

    def block(yy, zz, xx):
        return yy * 16 + zz * 4 + xx

    def a_at(q, zz, start=0, size=rows):
        return a.at[q, pl.ds(pl.multiple_of(zz * rows + start, 16), size)]

    def b_at(yy, zz, xx, start=0, size=rows):
        return b.at[pl.ds(pl.multiple_of(block(yy, zz, xx) * rows + start, half), size)]

    def chunk(ref, j):
        return ref.at[:, pl.ds(pl.multiple_of(j * wide, wide), wide)]

    def eye(count, first_row, first_col):
        r = lax.broadcasted_iota(jnp.int32, (count, tile), 0)
        k = lax.broadcasted_iota(jnp.int32, (count, tile), 1)
        return (r - k == first_col - first_row).astype(F32)

    def normalise(dst, src, masses, count, first_row, col, first_tile):
        height = src.shape[0]

        def step(t, _):
            at = pl.ds(pl.multiple_of(t * tile, tile), tile)
            there = pl.ds(pl.multiple_of((first_tile + t) * tile, tile), tile)
            value = src[:, at].astype(F32) + eye(height, first_row, col * cols + (first_tile + t) * tile)
            dst[:, at] = (value * inv[masses, :, there]).astype(BF16)
            return _

        lax.fori_loop(0, count, step, 0)

    def normalise_b(yy, zz, xx, src):
        normalise(b_at(yy, zz, xx), src, 0, wide // tile, block(yy, zz, xx) * rows, me.col, z * (wide // tile))

    def normalise_a(zz, src):
        normalise(a_at(q0, zz), src, 0, nt, block(yl, zz, x) * rows, me.col, 0)

    def landed_x(i, k, start=0, size=rows):
        if i == 0:
            return xraw.at[k, pl.ds(start, size)]
        yy, zz = pieces[i]
        return b_at(yy, zz, (xm, xp, x2)[k], start, size)

    def sent_x(i, k, start=0, size=rows):
        if i == 0:
            return xraw.at[k, pl.ds(start, size)]
        yy, zz = pieces[i]
        return b_at(yy, zz, x if k < 2 else (xm if start == 0 else xp), start, size)

    def spread_x(i, src):
        net.send(("bx+", i), src, sent_x(i, 0), me.dev(x=xp))
        net.send(("bx-", i), src, sent_x(i, 1), me.dev(x=xm))

    def forward_x(i):
        net.wait(("bx+", i), landed_x(i, 0), me.dev(x=xm))
        net.send(("bf+", i), landed_x(i, 0, 0, half), sent_x(i, 2, 0, half), me.dev(x=xp))
        net.wait(("bx-", i), landed_x(i, 1), me.dev(x=xp))
        net.send(("bf-", i), landed_x(i, 1, half, half), sent_x(i, 2, half, half), me.dev(x=xm))

    def last_x(i):
        net.need(("bf+", i), landed_x(i, 2, 0, half), me.dev(x=xm))
        net.need(("bf-", i), landed_x(i, 2, half, half), me.dev(x=xp))

    def start():
        for copy in fetch:
            copy.wait()
        for t in range(nt):
            at = slice(t * tile, (t + 1) * tile)
            on = (pattern[0, t] > 0).astype(F32)
            masked = flow[:, at].astype(F32) * on
            m[:, at] = masked.astype(BF16)
            masked = masked + eye(rows, me.row * rows, me.col * cols + t * tile)
            xs[x, :, at] = jnp.sum(masked, axis=0, keepdims=True)
            kept = jnp.logical_or(keep[0, t] > 0, me.row == me.col * nt + t).astype(F32)
            kx[:, at] = jnp.broadcast_to(kept, (8, tile))
        km[z] = kx[:, pl.ds(pl.multiple_of(z * wide, wide), wide)]
        ts[yl * 4 + x] = jnp.zeros(ts.shape[1:], F32)
        pl.semaphore_wait(barrier, len(peers))
        for d in (1, 3, 2):
            net.send(("mx", d), xs.at[x], xs.at[x], me.dev(x=(x + d) % 4))
        net.send("bz+", chunk(m, zp), braw.at[0], me.dev(z=zp))
        net.send("bz-", chunk(m, zm), braw.at[1], me.dev(z=zm))
        spread_x(0, chunk(m, z))

    def masses_x():
        for d in (1, 3, 2):
            src = (x - d + 4) % 4
            net.wait(("mx", d), xs.at[src], me.dev(x=src))
        here = yl * 4 + z
        zs[here] = (xs[0] + xs[1]) + (xs[2] + xs[3])
        for d, dy in around:
            net.send(("mz", d, dy), zs.at[here], zs.at[here], me.dev(z=(z + d) % 4, yl=(yl + dy) % 2))
        for p, (first, size) in enumerate(parts):
            at = pl.ds(first, size)
            net.send(("ay", p), m.at[at], yraw.at[at], across)
            if p == 0:
                net.send(("by", 0), chunk(m, z), craw, beside)
        net.send("bz2", chunk(m, z2), braw.at[2], me.dev(z=z2))
        for d in (1, 3, 2):
            net.send(("k", d), chunk(kx, (z + d) % 4), km.at[z], me.dev(z=(z + d) % 4))
        for first in (0, 1):
            for name, h, k, to in (("az0+", first, 0, zp), ("az0-", 1 - first, 1, zm)):
                at = pl.ds(h * half, half)
                net.send((name, h), m.at[at], araw.at[k, at], me.dev(z=to))

    def masses_z():
        for d, dy in around:
            zz, yy = (z - d + 4) % 4, (yl + dy) % 2
            net.wait(("mz", d, dy), zs.at[yy * 4 + zz], me.dev(z=zz, yl=yy))
        mass = ((zs[0] + zs[1]) + (zs[2] + zs[3])) + ((zs[4] + zs[5]) + (zs[6] + zs[7]))
        inv[0] = 1.0 / mass
        net.send("iv", inv.at[0], inv.at[1], across)

    def home(i):
        yy, zz = pieces[i]
        piece = b_at(yy, zz, x)
        if i in (1, 2, 3):
            name, k, src = {1: ("bz-", 1, zp), 2: ("bz+", 0, zm), 3: ("bz2", 2, z2)}[i]
            net.wait(name, braw.at[k], me.dev(z=src))
            normalise_b(yy, zz, x, braw.at[k])
            spread_x(i, piece)
            net.send(("by", i), piece, piece, beside)
        else:
            net.wait(("by", i - 4), craw if i == 4 else piece, beside)
            if i == 4:
                normalise_b(yy, zz, x, craw)
            spread_x(i, piece)

    def own_a():
        normalise_a(z, m)
        net.send(("ac0", 0), a_at(q0, z), a_at(q0, z), mate)

    def own_b():
        normalise_b(yl, z, x, chunk(m, z))
        c[...] = jnp.zeros(c.shape, F32)

    def raw_x():
        last_x(0)
        for k, xx in enumerate((xm, xp, x2)):
            normalise_b(yl, z, xx, xraw.at[k])

    def take_z0(k, h):
        at = pl.ds(h * half, half)
        if k == 0:
            net.need(("az0+", h), araw.at[0, at], me.dev(z=zm))
            if h == 0:
                net.send("af0+", araw.at[0, at], araw.at[2, at], me.dev(z=zp))
        elif k == 1:
            net.need(("az0-", h), araw.at[1, at], me.dev(z=zp))
            if h == 1:
                net.send("af0-", araw.at[1, at], araw.at[2, at], me.dev(z=zm))
        elif h == 0:
            net.need("af0+", araw.at[2, at], me.dev(z=zm))
        else:
            net.need("af0-", araw.at[2, at], me.dev(z=zp))

    def first_z0():
        take_z0(0, 0)
        take_z0(1, 1)

    def finish_z0(k):
        if k == 2:
            take_z0(2, 0)
            take_z0(2, 1)
        else:
            take_z0(k, 1 - k)
        zz = (zm, zp, z2)[k]
        normalise_a(zz, araw.at[k])
        start, size = parts[2]
        net.send(("ar", k), a_at(q0, zz, start, size), a_at(q0, zz, start, size), across)
        net.send(("ac0", k + 1), a_at(q0, zz), a_at(q0, zz), mate)

    def to_mate(k, p):
        zz = z_mates[k]
        net.send(("ac1", k, p), a_at(q1, zz, *parts[p]), a_at(q1, zz, *parts[p]), mate)

    def take_y(p):
        at = a_at(q1, z, *parts[p])
        first, size = parts[p]
        raw = yraw.at[pl.ds(first, size)]
        net.wait(("ay", p), raw, across)
        net.need("iv", inv.at[1], across)
        normalise(at, raw, 1, nt, block(yl, z, x) * rows + first, q1, 0)
        if p < 2:
            net.send(("az1+", p), at, at, me.dev(z=zp))
            net.send(("az1-", p), at, at, me.dev(z=zm))
        to_mate(0, p)

    def take_rest(k):
        net.wait(("ar", k), a_at(q1, (zm, zp, z2)[k], *parts[2]), across)
        to_mate(k + 1, 2)

    def take_z1(k, p):
        at = a_at(q1, (zm, zp, z2)[k], *parts[p])
        if k == 0:
            net.wait(("az1+", p), at, me.dev(z=zm))
            if p == 0:
                net.send("af1+", at, at, me.dev(z=zp))
        elif k == 1:
            net.wait(("az1-", p), at, me.dev(z=zp))
            if p == 1:
                net.send("af1-", at, at, me.dev(z=zm))
        elif p == 0:
            net.wait("af1+", at, me.dev(z=zm))
        else:
            net.wait("af1-", at, me.dev(z=zp))
        to_mate(k + 1, p)

    def first_z1():
        take_z1(0, 0)
        take_z1(1, 1)

    def ready_b(j):
        last_x(j)
        last_x(j + 4)

    def mate0():
        for k in range(4):
            net.need(("ac0", k), a_at(yh * 2 + 1 - core, z_mates[k]), mate)

    def mate1(k):
        for p in (0, 1, 2):
            net.need(("ac1", k, p), a_at((1 - yh) * 2 + 1 - core, z_mates[k], *parts[p]), mate)

    def units(yy, piece, ks):
        zi = z_order[piece]
        deep = 4 * rows
        left_at = pl.ds(pl.multiple_of((zi % 2) * deep, deep), deep)
        right_at = pl.ds(pl.multiple_of((yy * 4 + zi) * deep, deep), deep)
        q = yy * 2 + zi // 2

        def step(j, _):
            k, n = j // 2, j % 2
            zz = (z + (ks[0] if len(ks) == 1 else k if len(ks) == 4 else ks[0] + 2 * k)) % 4
            at = pl.ds(pl.multiple_of(n * 256, 256), 256)
            left = a[q, pl.ds(pl.multiple_of(zz * rows, rows), rows), left_at]
            value = jnp.dot(left, b[right_at, at], preferred_element_type=F32)
            c[zz, :, at] += value
            return _

        lax.fori_loop(0, 2 * len(ks), step, 0)

    def early(j):
        mate0()
        ready_b(j)
        units(yh, j, (0, 1, 2, 3))

    def late(j, ks):
        for k in ks:
            mate1({0: 0, 3: 1, 1: 2, 2: 3}[k])
        ready_b(j)
        units(1 - yh, j, ks)

    mine = yl * 4 + x

    def finish(d):
        zz = (z + d) % 4
        if d:
            net.need(("k", (4 - d) % 4), km.at[zz], me.dev(z=zz))
        for n in range(wide // 256):
            at = slice(n * 256, (n + 1) * 256)
            kept = c[zz, :, at] * km[zz, 0:1, at]
            ts[mine, :, at] += jnp.sum(kept * kept, axis=0, keepdims=True)
            top = jnp.max(kept, axis=0, keepdims=True)
            up = jnp.where(top > 0, 32767.0 / jnp.where(top > 0, top, 1.0), 0.0)
            cq[d, :, at] = jnp.round(kept * up).astype(jnp.int32).astype(jnp.int16)
            gsend[d, :, at] = top * (1.0 / 32767.0)
        if d:
            net.send(("c", d), cq.at[d], chunk(q_out, z), me.dev(z=zz))

    def total():
        own = pltpu.make_async_copy(cq.at[0], chunk(q_out, z), local_sem.at[0])
        own.start()
        for d, dy in around:
            net.send(("t", d, dy), ts.at[mine], ts.at[mine], me.dev(x=(x + d) % 4, yl=(yl + dy) % 2))
        for d, dy in around:
            xx, yy = (x - d + 4) % 4, (yl + dy) % 2
            net.wait(("t", d, dy), ts.at[yy * 4 + xx], me.dev(x=xx, yl=yy))
        whole = ((ts[0] + ts[1]) + (ts[2] + ts[3])) + ((ts[4] + ts[5]) + (ts[6] + ts[7]))
        scale = (rows * 32) / whole
        for d in range(4):
            gsend[d, :, wide:] = scale
        gs[z] = gsend[0]
        for d in (1, 3, 2):
            net.send(("s", d), gsend.at[d], gs.at[z], me.dev(z=(z + d) % 4))
        own.wait()
        for d in (1, 3, 2):
            src = (z - d + 4) % 4
            net.wait(("s", d), gs.at[src], me.dev(z=src))
        gs_out[...] = gs[...]
        for d in (1, 3, 2):
            src = (z - d + 4) % 4
            net.wait(("c", d), chunk(q_out, src), me.dev(z=src))
        net.drain()

    def later_z1():
        take_z1(0, 1)
        take_z1(1, 0)

    steps = {"start": start, "mx": masses_x, "inv": masses_z, "own": own_a, "nb0": own_b, "lx0": raw_x, "z0a": first_z0,
             "z1a": first_z1, "tot": total}
    for step in ORDER:
        if step in steps:
            steps[step]()
        elif step == "z1b":
            later_z1()
        elif step == "z1c":
            take_z1(2, 0)
            take_z1(2, 1)
        else:
            {"home": home, "f": forward_x, "y": take_y, "fin": finish_z0, "r": take_rest, "E": early, "C": finish,
             "Lz": lambda j: late(j, (0,)), "Lm": lambda j: late(j, (1, 3)), "L2": lambda j: late(j, (2,))}[step[0]](step[1])

def body(flow, pattern, keep):
    rows, cols = flow.shape
    tile = cols // pattern.shape[1]
    wide = cols // 4
    vmem = pl.BlockSpec(memory_space=pltpu.VMEM)
    anyspace = pl.BlockSpec(memory_space=pl.ANY)
    messages = 104
    coded, factors = pl.pallas_call(
        lambda *refs: kernel(tile, *refs),
        out_shape=(jax.ShapeDtypeStruct((rows, cols), jnp.int16), jax.ShapeDtypeStruct((4, 1, 2 * wide), F32)),
        in_specs=[pl.BlockSpec(memory_space=pltpu.HBM)] * 3,
        out_specs=(anyspace, vmem),
        scratch_shapes=[
            pltpu.VMEM((rows, cols), BF16),
            pltpu.SMEM(pattern.shape, jnp.int32),
            pltpu.SMEM(keep.shape, jnp.int32),
            pltpu.VMEM((4, 4 * rows, cols), BF16),
            pltpu.VMEM((32 * rows, wide), BF16),
            pltpu.VMEM((rows, cols), BF16),
            pltpu.VMEM((3, rows, cols), BF16),
            pltpu.VMEM((rows, cols), BF16),
            pltpu.VMEM((3, rows, wide), BF16),
            pltpu.VMEM((3, rows, wide), BF16),
            pltpu.VMEM((rows, wide), BF16),
            pltpu.VMEM((4, rows, wide), F32),
            pltpu.VMEM((4, rows, wide), jnp.int16),
            pltpu.VMEM((4, 1, cols), F32),
            pltpu.VMEM((8, 1, cols), F32),
            pltpu.VMEM((2, 1, cols), F32),
            pltpu.VMEM((8, cols), F32),
            pltpu.VMEM((4, 8, wide), F32),
            pltpu.VMEM((8, 1, wide), F32),
            pltpu.VMEM((4, 1, 2 * wide), F32),
            pltpu.VMEM((4, 1, 2 * wide), F32),
            pltpu.SemaphoreType.DMA((messages,)),
            pltpu.SemaphoreType.DMA((messages,)),
            pltpu.SemaphoreType.DMA((3,)),
        ],
        compiler_params=pltpu.CompilerParams(
            collective_id=0, has_side_effects=True, vmem_limit_bytes=52000 * 1024),
        name="cluster",
    )(*(pltpu.with_memory_space_constraint(v, pltpu.HBM) for v in (flow, pattern, keep)))
    down = factors[:, 0, :wide].reshape(1, cols)
    scale = factors[:, 0, wide:].reshape(1, cols)
    expanded = coded.astype(F32) * down
    return expanded * expanded * scale


def solution(mesh):
    return jax.shard_map(
        body,
        mesh=mesh,
        in_specs=(P("row", "col"), P("row", "col"), P("row", "col")),
        out_specs=P("row", "col"),
        check_vma=False,
    )
```

time: 115 us -> 105 us (0.913)
  Pallas kernels: 110 us -> 102 us
  local copies, waits for them, and re-layouts: 2.54 us -> 0.01 us
    pallas_call x1, Pallas kernels: 110 us -> 102 us  [body(): pl.pallas_call(lambda *refs: kernel(tile, *refs), out_shape=(jax.ShapeDty...]
    unnamed x6 -> x0, local copies, waits for them, and re-layouts: 2.53 us -> none
where the time goes in v3:
time: 105 us; the launch traced here: 104 us
  Pallas kernels  102 us (97%)
  other arithmetic  1.83 us (2%)
    pallas_call x1, Pallas kernels, body(): pl.pallas_call(lambda *refs: kernel(tile, *refs), out_shape=(jax.ShapeDty...  102 us

profile of v3, /device:TPU:0, one launch (start us, length us, event | category | flops | bytes accessed | tf_op | source)
XLA Modules:
  0.0 104.3 jit_solution(18052842510749574483)
XLA Ops:
  0.0 102.5 %cluster.1 = (s16[256,2048]{1,0:T(8,128)(2,1)S(1)}, f32[4,1,1024]{2,1,0:T(1,128)S(1)}) custom-call(bf16[256,2048]{1,0:T(8,128)(2,1)} %refs_0_.1, s32[1,8]{1,0:T(1,128)} %refs_1_.1, s32[1,8]{1,0:T(1,128)} %refs_2_.1), custom_call_target="tpu_custom_call" | custom-call | tf_op jit(solution)/shard_map/cluster/pallas_call | solution.py:418
  102.5 1.8 %multiply_multiply_fusion = f32[256,2048]{1,0:T(8,128)} fusion(s16[256,2048]{1,0:T(8,128)(2,1)S(1)} %get-tuple-element.7, f32[2048]{0:T(1024)S(1)} %bitcast.3, f32[2048]{0:T(1024)S(1)} %bitcast.2), kind=kLoop, calls=%fused_computation | loop fusion | flops 2097152 | bytes 3162112 | tf_op jit(solution)/shard_map/mul | solution.py:456
  (1 shorter events, 0.0 us)

commit v4 on v3

--- a/solution.py
+++ b/solution.py
@@ -8,14 +8,13 @@
 MESH = pl.DeviceIdType.MESH
 F32 = jnp.float32
 BF16 = jnp.bfloat16
-RING = 6
+RING = 7
 ORDER = (
-    "start", "mx", ("f", 0), "inv", ("home", 1), ("home", 2), "own", "nb0", "lx0", ("home", 3), ("f", 1), ("home", 4),
-    ("f", 2), "z0a", ("f", 3), ("y", 0), ("y", 1), ("y", 2), ("fin", 0), ("f", 4), ("fin", 1), ("home", 5),
-    ("home", 6), ("Lz", 0), ("fin", 2), ("home", 7), ("f", 5), ("E", 0), "z1a", ("r", 0), ("f", 6), ("r", 1),
-    ("f", 7), "z1b", ("E", 1), ("Lz", 1), ("Lm", 0), ("r", 2), ("Lm", 1), ("E", 2), ("Lz", 2), ("Lm", 2), "z1c",
-    ("E", 3), ("Lz", 3), ("Lm", 3), ("C", 1), ("C", 3), ("L2", 0), ("L2", 1), ("L2", 2), ("L2", 3), ("C", 2),
-    ("C", 0), "tot",
+    "start", "mx", ("f", 0), "inv", ("home", 1), ("home", 2), "own", "nb0", "lx0", "z0f", ("f", 1), "z0a",
+    ("home", 4), ("home", 3), ("f", 2), "z0b", ("fin", 0), ("fin", 1), ("f", 4), ("y", 0), ("y", 1), ("y", 2),
+    ("fin", 2), ("f", 3), ("home", 5), ("home", 6), ("E", 0), "z1a", ("home", 7), ("f", 5), ("r", 0), "z1b", ("r", 1),
+    ("f", 6), ("r", 2), ("L", 0), ("f", 7), ("E", 1), "z1c", ("L", 1), ("E", 2), ("L", 2), ("E", 3), ("O", 0),
+    ("O", 1), ("O", 2), ("L", 3), ("O", 3), ("C", 1), ("C", 3), ("C", 2), ("C", 0), "tot",
 )
 
 
@@ -67,7 +66,7 @@
             copy.wait_send()
 
 
-def kernel(tile, flow_hbm, pattern_hbm, keep_hbm, q_out, gs_out, flow, pattern, keep, a, b, m, araw, yraw, braw, xraw, craw, c, cq,
+def kernel(tile, flow_hbm, pattern_hbm, keep_hbm, q_out, gs_out, flow, pattern, keep, a, b, m, araw, yraw, xraw, craw, c, cq,
            xs, zs, inv, kx, km, ts, gsend, gs, send_sem, recv_sem, local_sem):
     me = Place()
     rows, cols = flow.shape
@@ -100,8 +99,8 @@
     def block(yy, zz, xx):
         return yy * 16 + zz * 4 + xx
 
-    def a_at(q, zz, start=0, size=rows):
-        return a.at[q, pl.ds(pl.multiple_of(zz * rows + start, 16), size)]
+    def a_at(q, k, start=0, size=rows):
+        return a.at[q, pl.ds(k * rows + start, size)]
 
     def b_at(yy, zz, xx, start=0, size=rows):
         return b.at[pl.ds(pl.multiple_of(block(yy, zz, xx) * rows + start, half), size)]
@@ -129,8 +128,8 @@
     def normalise_b(yy, zz, xx, src):
         normalise(b_at(yy, zz, xx), src, 0, wide // tile, block(yy, zz, xx) * rows, me.col, z * (wide // tile))
 
-    def normalise_a(zz, src):
-        normalise(a_at(q0, zz), src, 0, nt, block(yl, zz, x) * rows, me.col, 0)
+    def normalise_a(k, src):
+        normalise(a_at(q0, k), src, 0, nt, block(yl, z_mates[k], x) * rows, me.col, 0)
 
     def landed_x(i, k, start=0, size=rows):
         if i == 0:
@@ -166,17 +165,16 @@
             on = (pattern[0, t] > 0).astype(F32)
             masked = flow[:, at].astype(F32) * on
             m[:, at] = masked.astype(BF16)
-            masked = masked + eye(rows, me.row * rows, me.col * cols + t * tile)
-            xs[x, :, at] = jnp.sum(masked, axis=0, keepdims=True)
-            kept = jnp.logical_or(keep[0, t] > 0, me.row == me.col * nt + t).astype(F32)
+            diagonal = me.row == me.col * nt + t
+            xs[x, :, at] = jnp.sum(masked, axis=0, keepdims=True) + diagonal.astype(F32)
+            kept = jnp.logical_or(keep[0, t] > 0, diagonal).astype(F32)
             kx[:, at] = jnp.broadcast_to(kept, (8, tile))
         km[z] = kx[:, pl.ds(pl.multiple_of(z * wide, wide), wide)]
         ts[yl * 4 + x] = jnp.zeros(ts.shape[1:], F32)
         pl.semaphore_wait(barrier, len(peers))
         for d in (1, 3, 2):
             net.send(("mx", d), xs.at[x], xs.at[x], me.dev(x=(x + d) % 4))
-        net.send("bz+", chunk(m, zp), braw.at[0], me.dev(z=zp))
-        net.send("bz-", chunk(m, zm), braw.at[1], me.dev(z=zm))
+        send_z0(0)
         spread_x(0, chunk(m, z))
 
     def masses_x():
@@ -192,13 +190,10 @@
             net.send(("ay", p), m.at[at], yraw.at[at], across)
             if p == 0:
                 net.send(("by", 0), chunk(m, z), craw, beside)
-        net.send("bz2", chunk(m, z2), braw.at[2], me.dev(z=z2))
         for d in (1, 3, 2):
             net.send(("k", d), chunk(kx, (z + d) % 4), km.at[z], me.dev(z=(z + d) % 4))
-        for first in (0, 1):
-            for name, h, k, to in (("az0+", first, 0, zp), ("az0-", 1 - first, 1, zm)):
-                at = pl.ds(h * half, half)
-                net.send((name, h), m.at[at], araw.at[k, at], me.dev(z=to))
+        send_z0(1)
+        send_z0(2)
 
     def masses_z():
         for d, dy in around:
@@ -212,9 +207,12 @@
         yy, zz = pieces[i]
         piece = b_at(yy, zz, x)
         if i in (1, 2, 3):
-            name, k, src = {1: ("bz-", 1, zp), 2: ("bz+", 0, zm), 3: ("bz2", 2, z2)}[i]
-            net.wait(name, braw.at[k], me.dev(z=src))
-            normalise_b(yy, zz, x, braw.at[k])
+            k = {1: 1, 2: 0, 3: 2}[i]
+            if k < 2:
+                take_z0(k, 0)
+            else:
+                last_z0(0)
+            normalise_b(yy, zz, x, chunk(araw.at[k], z))
             spread_x(i, piece)
             net.send(("by", i), piece, piece, beside)
         else:
@@ -224,8 +222,8 @@
             spread_x(i, piece)
 
     def own_a():
-        normalise_a(z, m)
-        net.send(("ac0", 0), a_at(q0, z), a_at(q0, z), mate)
+        normalise_a(0, m)
+        net.send(("ac0", 0), a_at(q0, 0), a_at(q0, 0), mate)
 
     def own_b():
         normalise_b(yl, z, x, chunk(m, z))
@@ -236,67 +234,80 @@
         for k, xx in enumerate((xm, xp, x2)):
             normalise_b(yl, z, xx, xraw.at[k])
 
-    def take_z0(k, h):
-        at = pl.ds(h * half, half)
+    plus, minus = (zp, z2, z, zm), (zm, z2, z, zp)
+
+    def send_z0(n):
+        net.send(("az0+", n), chunk(m, plus[n]), chunk(araw.at[0], plus[n]), me.dev(z=zp))
+        net.send(("az0-", n), chunk(m, minus[n]), chunk(araw.at[1], minus[n]), me.dev(z=zm))
+
+    def take_z0(k, n):
         if k == 0:
-            net.need(("az0+", h), araw.at[0, at], me.dev(z=zm))
-            if h == 0:
-                net.send("af0+", araw.at[0, at], araw.at[2, at], me.dev(z=zp))
-        elif k == 1:
-            net.need(("az0-", h), araw.at[1, at], me.dev(z=zp))
-            if h == 1:
-                net.send("af0-", araw.at[1, at], araw.at[2, at], me.dev(z=zm))
-        elif h == 0:
-            net.need("af0+", araw.at[2, at], me.dev(z=zm))
+            net.need(("az0+", n), chunk(araw.at[0], (z, zp, zm, z2)[n]), me.dev(z=zm))
         else:
-            net.need("af0-", araw.at[2, at], me.dev(z=zp))
+            net.need(("az0-", n), chunk(araw.at[1], (z, zm, zp, z2)[n]), me.dev(z=zp))
+
+    def rows_of(ref, h):
+        return ref.at[pl.ds(h * half, half)]
+
+    def forward_z0(n):
+        take_z0(0, n)
+        j = (z, zp, zm, z2)[n]
+        net.send(("af0+", n), rows_of(chunk(araw.at[0], j), 0), rows_of(chunk(araw.at[2], j), 0), me.dev(z=zp))
+        take_z0(1, n)
+        j = (z, zm, zp, z2)[n]
+        net.send(("af0-", n), rows_of(chunk(araw.at[1], j), 1), rows_of(chunk(araw.at[2], j), 1), me.dev(z=zm))
+
+    def last_z0(f):
+        n = (1, 0, 2, 3)[f]
+        net.need(("af0+", n), rows_of(chunk(araw.at[2], (zm, z, z2, zp)[n]), 0), me.dev(z=zm))
+        net.need(("af0-", n), rows_of(chunk(araw.at[2], (zp, z, z2, zm)[n]), 1), me.dev(z=zp))
 
     def first_z0():
-        take_z0(0, 0)
-        take_z0(1, 1)
+        forward_z0(1)
+        send_z0(3)
+
+    def middle_z0():
+        forward_z0(0)
+        forward_z0(2)
 
     def finish_z0(k):
         if k == 2:
-            take_z0(2, 0)
-            take_z0(2, 1)
-        else:
-            take_z0(k, 1 - k)
-        zz = (zm, zp, z2)[k]
-        normalise_a(zz, araw.at[k])
-        start, size = parts[2]
-        net.send(("ar", k), a_at(q0, zz, start, size), a_at(q0, zz, start, size), across)
-        net.send(("ac0", k + 1), a_at(q0, zz), a_at(q0, zz), mate)
+            for f in range(4):
+                last_z0(f)
+        normalise_a(k + 1, araw.at[k])
+        rest = a_at(q0, k + 1, *parts[2])
+        net.send(("ar", k), rest, rest, across)
+        net.send(("ac0", k + 1), a_at(q0, k + 1), a_at(q0, k + 1), mate)
 
     def to_mate(k, p):
-        zz = z_mates[k]
-        net.send(("ac1", k, p), a_at(q1, zz, *parts[p]), a_at(q1, zz, *parts[p]), mate)
+        net.send(("ac1", k, p), a_at(q1, k, *parts[p]), a_at(q1, k, *parts[p]), mate)
 
     def take_y(p):
-        at = a_at(q1, z, *parts[p])
+        at = a_at(q1, 0, *parts[p])
         first, size = parts[p]
         raw = yraw.at[pl.ds(first, size)]
         net.wait(("ay", p), raw, across)
         net.need("iv", inv.at[1], across)
         normalise(at, raw, 1, nt, block(yl, z, x) * rows + first, q1, 0)
         if p < 2:
-            net.send(("az1+", p), at, at, me.dev(z=zp))
-            net.send(("az1-", p), at, at, me.dev(z=zm))
+            net.send(("az1+", p), at, a_at(q1, 1, *parts[p]), me.dev(z=zp))
+            net.send(("az1-", p), at, a_at(q1, 2, *parts[p]), me.dev(z=zm))
         to_mate(0, p)
 
     def take_rest(k):
-        net.wait(("ar", k), a_at(q1, (zm, zp, z2)[k], *parts[2]), across)
+        net.wait(("ar", k), a_at(q1, k + 1, *parts[2]), across)
         to_mate(k + 1, 2)
 
     def take_z1(k, p):
-        at = a_at(q1, (zm, zp, z2)[k], *parts[p])
+        at = a_at(q1, k + 1, *parts[p])
         if k == 0:
             net.wait(("az1+", p), at, me.dev(z=zm))
             if p == 0:
-                net.send("af1+", at, at, me.dev(z=zp))
+                net.send("af1+", at, a_at(q1, 3, *parts[p]), me.dev(z=zp))
         elif k == 1:
             net.wait(("az1-", p), at, me.dev(z=zp))
             if p == 1:
-                net.send("af1-", at, at, me.dev(z=zm))
+                net.send("af1-", at, a_at(q1, 3, *parts[p]), me.dev(z=zm))
         elif p == 0:
             net.wait("af1+", at, me.dev(z=zm))
         else:
@@ -313,40 +324,29 @@
 
     def mate0():
         for k in range(4):
-            net.need(("ac0", k), a_at(yh * 2 + 1 - core, z_mates[k]), mate)
+            net.need(("ac0", k), a_at(yh * 2 + 1 - core, k), mate)
 
     def mate1(k):
         for p in (0, 1, 2):
-            net.need(("ac1", k, p), a_at((1 - yh) * 2 + 1 - core, z_mates[k], *parts[p]), mate)
-
-    def units(yy, piece, ks):
+            net.need(("ac1", k, p), a_at((1 - yh) * 2 + 1 - core, k, *parts[p]), mate)
+
+    def units(yy, piece, first, count):
         zi = z_order[piece]
         deep = 4 * rows
-        left_at = pl.ds(pl.multiple_of((zi % 2) * deep, deep), deep)
-        right_at = pl.ds(pl.multiple_of((yy * 4 + zi) * deep, deep), deep)
-        q = yy * 2 + zi // 2
-
-        def step(j, _):
-            k, n = j // 2, j % 2
-            zz = (z + (ks[0] if len(ks) == 1 else k if len(ks) == 4 else ks[0] + 2 * k)) % 4
-            at = pl.ds(pl.multiple_of(n * 256, 256), 256)
-            left = a[q, pl.ds(pl.multiple_of(zz * rows, rows), rows), left_at]
-            value = jnp.dot(left, b[right_at, at], preferred_element_type=F32)
-            c[zz, :, at] += value
-            return _
-
-        lax.fori_loop(0, 2 * len(ks), step, 0)
+        left = a[yy * 2 + zi // 2, pl.ds(first * rows, count * rows), pl.ds(pl.multiple_of((zi % 2) * deep, deep), deep)]
+        right = b[pl.ds(pl.multiple_of((yy * 4 + zi) * deep, deep), deep)]
+        c[pl.ds(first * rows, count * rows)] += jnp.dot(left, right, preferred_element_type=F32)
 
     def early(j):
         mate0()
         ready_b(j)
-        units(yh, j, (0, 1, 2, 3))
-
-    def late(j, ks):
-        for k in ks:
-            mate1({0: 0, 3: 1, 1: 2, 2: 3}[k])
+        units(yh, j, 0, 4)
+
+    def late(j, first, count):
+        for k in range(first, first + count):
+            mate1(k)
         ready_b(j)
-        units(1 - yh, j, ks)
+        units(1 - yh, j, first, count)
 
     mine = yl * 4 + x
 
@@ -354,14 +354,13 @@
         zz = (z + d) % 4
         if d:
             net.need(("k", (4 - d) % 4), km.at[zz], me.dev(z=zz))
-        for n in range(wide // 256):
-            at = slice(n * 256, (n + 1) * 256)
-            kept = c[zz, :, at] * km[zz, 0:1, at]
-            ts[mine, :, at] += jnp.sum(kept * kept, axis=0, keepdims=True)
-            top = jnp.max(kept, axis=0, keepdims=True)
-            up = jnp.where(top > 0, 32767.0 / jnp.where(top > 0, top, 1.0), 0.0)
-            cq[d, :, at] = jnp.round(kept * up).astype(jnp.int32).astype(jnp.int16)
-            gsend[d, :, at] = top * (1.0 / 32767.0)
+        slot = (0, 2, 3, 1)[d]
+        kept = c[slot * rows:(slot + 1) * rows] * km[zz, 0:1]
+        ts[mine] += jnp.sum(kept * kept, axis=0, keepdims=True)
+        top = jnp.max(kept, axis=0, keepdims=True)
+        up = jnp.where(top > 0, 32767.0 / jnp.where(top > 0, top, 1.0), 0.0)
+        cq[d] = jnp.round(kept * up).astype(jnp.int32).astype(jnp.int16)
+        gsend[d, :, :wide] = top * (1.0 / 32767.0)
         if d:
             net.send(("c", d), cq.at[d], chunk(q_out, z), me.dev(z=zz))
 
@@ -394,8 +393,8 @@
         take_z1(0, 1)
         take_z1(1, 0)
 
-    steps = {"start": start, "mx": masses_x, "inv": masses_z, "own": own_a, "nb0": own_b, "lx0": raw_x, "z0a": first_z0,
-             "z1a": first_z1, "tot": total}
+    steps = {"start": start, "mx": masses_x, "inv": masses_z, "own": own_a, "nb0": own_b, "lx0": raw_x, "z0f": first_z0,
+             "z0a": middle_z0, "z0b": lambda: forward_z0(3), "z1a": first_z1, "tot": total}
     for step in ORDER:
         if step in steps:
             steps[step]()
@@ -406,7 +405,7 @@
             take_z1(2, 1)
         else:
             {"home": home, "f": forward_x, "y": take_y, "fin": finish_z0, "r": take_rest, "E": early, "C": finish,
-             "Lz": lambda j: late(j, (0,)), "Lm": lambda j: late(j, (1, 3)), "L2": lambda j: late(j, (2,))}[step[0]](step[1])
+             "L": lambda j: late(j, 0, 3), "O": lambda j: late(j, 3, 1)}[step[0]](step[1])
 
 def body(flow, pattern, keep):
     rows, cols = flow.shape
@@ -414,7 +413,7 @@
     wide = cols // 4
     vmem = pl.BlockSpec(memory_space=pltpu.VMEM)
     anyspace = pl.BlockSpec(memory_space=pl.ANY)
-    messages = 104
+    messages = 112
     coded, factors = pl.pallas_call(
         lambda *refs: kernel(tile, *refs),
         out_shape=(jax.ShapeDtypeStruct((rows, cols), jnp.int16), jax.ShapeDtypeStruct((4, 1, 2 * wide), F32)),
@@ -430,9 +429,8 @@
             pltpu.VMEM((3, rows, cols), BF16),
             pltpu.VMEM((rows, cols), BF16),
             pltpu.VMEM((3, rows, wide), BF16),
-            pltpu.VMEM((3, rows, wide), BF16),
             pltpu.VMEM((rows, wide), BF16),
-            pltpu.VMEM((4, rows, wide), F32),
+            pltpu.VMEM((4 * rows, wide), F32),
             pltpu.VMEM((4, rows, wide), jnp.int16),
             pltpu.VMEM((4, 1, cols), F32),
             pltpu.VMEM((8, 1, cols), F32),

time: 105 us -> 98.5 us (0.938)
  Pallas kernels: 102 us -> 96.5 us
    pallas_call x1, Pallas kernels: 102 us -> 96.5 us  [body(): pl.pallas_call(lambda *refs: kernel(tile, *refs), out_shape=(jax.ShapeDty...]
where the time goes in v4:
time: 98.5 us; the launch traced here: 98.3 us
  Pallas kernels  96.5 us (98%)
  other arithmetic  1.83 us (2%)
    pallas_call x1, Pallas kernels, body(): pl.pallas_call(lambda *refs: kernel(tile, *refs), out_shape=(jax.ShapeDty...  96.5 us

profile of v4, /device:TPU:0, one launch (start us, length us, event | category | flops | bytes accessed | tf_op | source)
XLA Modules:
  0.0 98.3 jit_solution(4094518200529394659)
XLA Ops:
  0.0 96.5 %cluster.1 = (s16[256,2048]{1,0:T(8,128)(2,1)S(1)}, f32[4,1,1024]{2,1,0:T(1,128)S(1)}) custom-call(bf16[256,2048]{1,0:T(8,128)(2,1)} %refs_0_.1, s32[1,8]{1,0:T(1,128)} %refs_1_.1, s32[1,8]{1,0:T(1,128)} %refs_2_.1), custom_call_target="tpu_custom_call" | custom-call | tf_op jit(solution)/shard_map/cluster/pallas_call | solution.py:417
  96.5 1.8 %multiply_multiply_fusion = f32[256,2048]{1,0:T(8,128)} fusion(s16[256,2048]{1,0:T(8,128)(2,1)S(1)} %get-tuple-element.7, f32[2048]{0:T(1024)S(1)} %bitcast.3, f32[2048]{0:T(1024)S(1)} %bitcast.2), kind=kLoop, calls=%fused_computation | loop fusion | flops 2097152 | bytes 3162112 | tf_op jit(solution)/shard_map/mul | solution.py:454
  (1 shorter events, 0.0 us)

commit v5 on v4

--- a/solution.py
+++ b/solution.py
@@ -10,11 +10,17 @@
 BF16 = jnp.bfloat16
 RING = 7
 ORDER = (
-    "start", "mx", ("f", 0), "inv", ("home", 1), ("home", 2), "own", "nb0", "lx0", "z0f", ("f", 1), "z0a",
-    ("home", 4), ("home", 3), ("f", 2), "z0b", ("fin", 0), ("fin", 1), ("f", 4), ("y", 0), ("y", 1), ("y", 2),
-    ("fin", 2), ("f", 3), ("home", 5), ("home", 6), ("E", 0), "z1a", ("home", 7), ("f", 5), ("r", 0), "z1b", ("r", 1),
-    ("f", 6), ("r", 2), ("L", 0), ("f", 7), ("E", 1), "z1c", ("L", 1), ("E", 2), ("L", 2), ("E", 3), ("O", 0),
-    ("O", 1), ("O", 2), ("L", 3), ("O", 3), ("C", 1), ("C", 3), ("C", 2), ("C", 0), "tot",
+    ("start",), ("mx",), ("sb", 0), ("sb", 1), ("sy", 1), ("f", 0, 0), ("f", 0, 1), ("inv",), ("home", 4, 0),
+    ("home", 2, 1), ("g", 0), ("home", 1, 0), ("g", 1), ("own",), ("sa", 2), ("home", 4, 1), ("sa", 3),
+    ("home", 3, 1), ("sy", 0), ("y", 1), ("f", 1, 0), ("g", 2), ("home", 3, 0), ("home", 5, 0), ("f", 4, 1),
+    ("lx", 1), ("home", 2, 0), ("fin", 0), ("fin", 1), ("home", 7, 1), ("home", 1, 1), ("g", 3), ("lx", 0), ("sy", 2),
+    ("f", 7, 1), ("f", 2, 0), ("f", 5, 0), ("y", 0), ("f", 1, 1), ("nb0",), ("z1", 1), ("f", 4, 0), ("f", 3, 1),
+    ("home", 7, 0), ("fin", 2), ("f", 3, 0), ("r", 1), ("home", 6, 0), ("z1", 0), ("f", 7, 0), ("E", 1, 0),
+    ("home", 6, 1), ("E", 0, 0), ("E", 0, 1), ("f", 6, 0), ("r", 0), ("y", 2), ("E", 3, 1), ("home", 5, 1), ("zo", 1),
+    ("L", 1, 0), ("r", 2), ("L", 3, 0), ("f", 6, 1), ("E", 3, 0), ("L", 2, 0), ("L", 0, 0), ("f", 2, 1), ("zo", 0),
+    ("E", 2, 0), ("C", 1, 0), ("C", 0, 0), ("f", 5, 1), ("L", 3, 1), ("L", 0, 1), ("O", 2, 0), ("O", 1, 0),
+    ("O", 0, 0), ("O", 3, 0), ("C", 2, 0), ("O", 2, 1), ("O", 3, 1), ("O", 0, 1), ("E", 2, 1), ("O", 1, 1),
+    ("E", 1, 1), ("C", 2, 1), ("L", 2, 1), ("L", 1, 1), ("C", 0, 1), ("C", 1, 1), ("tot",),
 )
 
 
@@ -73,6 +79,7 @@
     nt = cols // tile
     half = rows // 2
     wide = cols // 4
+    side = wide // 2
     ring = RING * rows // 8
     parts = ((0, ring // 2), (ring // 2, ring // 2), (ring, rows - ring))
     x, z, yl, yh, core = me.x, me.z, me.yl, me.yh, me.c
@@ -102,11 +109,14 @@
     def a_at(q, k, start=0, size=rows):
         return a.at[q, pl.ds(k * rows + start, size)]
 
-    def b_at(yy, zz, xx, start=0, size=rows):
-        return b.at[pl.ds(pl.multiple_of(block(yy, zz, xx) * rows + start, half), size)]
+    def b_at(n, yy, zz, xx, start=0, size=rows):
+        return b.at[n, pl.ds(pl.multiple_of(block(yy, zz, xx) * rows + start, half), size)]
 
     def chunk(ref, j):
         return ref.at[:, pl.ds(pl.multiple_of(j * wide, wide), wide)]
+
+    def half_chunk(ref, j, n):
+        return ref.at[:, pl.ds(pl.multiple_of(j * wide + n * side, side), side)]
 
     def eye(count, first_row, first_col):
         r = lax.broadcasted_iota(jnp.int32, (count, tile), 0)
@@ -125,37 +135,38 @@
 
         lax.fori_loop(0, count, step, 0)
 
-    def normalise_b(yy, zz, xx, src):
-        normalise(b_at(yy, zz, xx), src, 0, wide // tile, block(yy, zz, xx) * rows, me.col, z * (wide // tile))
+    def normalise_b(n, yy, zz, xx, src):
+        count = side // tile
+        normalise(b_at(n, yy, zz, xx), src, 0, count, block(yy, zz, xx) * rows, me.col, (2 * z + n) * count)
 
     def normalise_a(k, src):
         normalise(a_at(q0, k), src, 0, nt, block(yl, z_mates[k], x) * rows, me.col, 0)
 
-    def landed_x(i, k, start=0, size=rows):
+    def landed_x(i, n, k, start=0, size=rows):
         if i == 0:
-            return xraw.at[k, pl.ds(start, size)]
+            return xraw.at[k, n, pl.ds(start, size)]
         yy, zz = pieces[i]
-        return b_at(yy, zz, (xm, xp, x2)[k], start, size)
-
-    def sent_x(i, k, start=0, size=rows):
+        return b_at(n, yy, zz, (xm, xp, x2)[k], start, size)
+
+    def sent_x(i, n, k, start=0, size=rows):
         if i == 0:
-            return xraw.at[k, pl.ds(start, size)]
+            return xraw.at[k, n, pl.ds(start, size)]
         yy, zz = pieces[i]
-        return b_at(yy, zz, x if k < 2 else (xm if start == 0 else xp), start, size)
-
-    def spread_x(i, src):
-        net.send(("bx+", i), src, sent_x(i, 0), me.dev(x=xp))
-        net.send(("bx-", i), src, sent_x(i, 1), me.dev(x=xm))
-
-    def forward_x(i):
-        net.wait(("bx+", i), landed_x(i, 0), me.dev(x=xm))
-        net.send(("bf+", i), landed_x(i, 0, 0, half), sent_x(i, 2, 0, half), me.dev(x=xp))
-        net.wait(("bx-", i), landed_x(i, 1), me.dev(x=xp))
-        net.send(("bf-", i), landed_x(i, 1, half, half), sent_x(i, 2, half, half), me.dev(x=xm))
-
-    def last_x(i):
-        net.need(("bf+", i), landed_x(i, 2, 0, half), me.dev(x=xm))
-        net.need(("bf-", i), landed_x(i, 2, half, half), me.dev(x=xp))
+        return b_at(n, yy, zz, x if k < 2 else (xm if start == 0 else xp), start, size)
+
+    def spread_x(i, n, src):
+        net.send(("bx+", i, n), src, sent_x(i, n, 0), me.dev(x=xp))
+        net.send(("bx-", i, n), src, sent_x(i, n, 1), me.dev(x=xm))
+
+    def forward_x(i, n):
+        net.wait(("bx+", i, n), landed_x(i, n, 0), me.dev(x=xm))
+        net.send(("bf+", i, n), landed_x(i, n, 0, 0, half), sent_x(i, n, 2, 0, half), me.dev(x=xp))
+        net.wait(("bx-", i, n), landed_x(i, n, 1), me.dev(x=xp))
+        net.send(("bf-", i, n), landed_x(i, n, 1, half, half), sent_x(i, n, 2, half, half), me.dev(x=xm))
+
+    def last_x(i, n):
+        net.need(("bf+", i, n), landed_x(i, n, 2, 0, half), me.dev(x=xm))
+        net.need(("bf-", i, n), landed_x(i, n, 2, half, half), me.dev(x=xp))
 
     def start():
         for copy in fetch:
@@ -175,7 +186,8 @@
         for d in (1, 3, 2):
             net.send(("mx", d), xs.at[x], xs.at[x], me.dev(x=(x + d) % 4))
         send_z0(0)
-        spread_x(0, chunk(m, z))
+        for n in (0, 1):
+            spread_x(0, n, half_chunk(m, z, n))
 
     def masses_x():
         for d in (1, 3, 2):
@@ -185,15 +197,16 @@
         zs[here] = (xs[0] + xs[1]) + (xs[2] + xs[3])
         for d, dy in around:
             net.send(("mz", d, dy), zs.at[here], zs.at[here], me.dev(z=(z + d) % 4, yl=(yl + dy) % 2))
-        for p, (first, size) in enumerate(parts):
-            at = pl.ds(first, size)
-            net.send(("ay", p), m.at[at], yraw.at[at], across)
-            if p == 0:
-                net.send(("by", 0), chunk(m, z), craw, beside)
         for d in (1, 3, 2):
             net.send(("k", d), chunk(kx, (z + d) % 4), km.at[z], me.dev(z=(z + d) % 4))
         send_z0(1)
-        send_z0(2)
+
+    def send_y(p):
+        at = pl.ds(parts[p][0], parts[p][1])
+        net.send(("ay", p), m.at[at], yraw.at[at], across)
+
+    def send_b(n):
+        net.send(("by", 0, n), half_chunk(m, z, n), craw.at[n], beside)
 
     def masses_z():
         for d, dy in around:
@@ -203,36 +216,36 @@
         inv[0] = 1.0 / mass
         net.send("iv", inv.at[0], inv.at[1], across)
 
-    def home(i):
+    def home(i, n):
         yy, zz = pieces[i]
-        piece = b_at(yy, zz, x)
-        if i in (1, 2, 3):
+        piece = b_at(n, yy, zz, x)
+        if i < 4:
             k = {1: 1, 2: 0, 3: 2}[i]
             if k < 2:
                 take_z0(k, 0)
             else:
                 last_z0(0)
-            normalise_b(yy, zz, x, chunk(araw.at[k], z))
-            spread_x(i, piece)
-            net.send(("by", i), piece, piece, beside)
+            normalise_b(n, yy, zz, x, half_chunk(araw.at[k], z, n))
+            net.send(("by", i, n), piece, piece, beside)
         else:
-            net.wait(("by", i - 4), craw if i == 4 else piece, beside)
+            net.wait(("by", i - 4, n), craw.at[n] if i == 4 else piece, beside)
             if i == 4:
-                normalise_b(yy, zz, x, craw)
-            spread_x(i, piece)
+                normalise_b(n, yy, zz, x, craw.at[n])
+        spread_x(i, n, piece)
 
     def own_a():
         normalise_a(0, m)
         net.send(("ac0", 0), a_at(q0, 0), a_at(q0, 0), mate)
 
     def own_b():
-        normalise_b(yl, z, x, chunk(m, z))
+        for n in (0, 1):
+            normalise_b(n, yl, z, x, half_chunk(m, z, n))
         c[...] = jnp.zeros(c.shape, F32)
 
-    def raw_x():
-        last_x(0)
+    def raw_x(n):
+        last_x(0, n)
         for k, xx in enumerate((xm, xp, x2)):
-            normalise_b(yl, z, xx, xraw.at[k])
+            normalise_b(n, yl, z, xx, xraw.at[k, n])
 
     plus, minus = (zp, z2, z, zm), (zm, z2, z, zp)
 
@@ -262,18 +275,12 @@
         net.need(("af0+", n), rows_of(chunk(araw.at[2], (zm, z, z2, zp)[n]), 0), me.dev(z=zm))
         net.need(("af0-", n), rows_of(chunk(araw.at[2], (zp, z, z2, zm)[n]), 1), me.dev(z=zp))
 
-    def first_z0():
-        forward_z0(1)
-        send_z0(3)
-
-    def middle_z0():
-        forward_z0(0)
-        forward_z0(2)
-
     def finish_z0(k):
-        if k == 2:
-            for f in range(4):
-                last_z0(f)
+        for n in range(4):
+            if k == 2:
+                last_z0(n)
+            else:
+                take_z0(k, n)
         normalise_a(k + 1, araw.at[k])
         rest = a_at(q0, k + 1, *parts[2])
         net.send(("ar", k), rest, rest, across)
@@ -298,29 +305,27 @@
         net.wait(("ar", k), a_at(q1, k + 1, *parts[2]), across)
         to_mate(k + 1, 2)
 
-    def take_z1(k, p):
-        at = a_at(q1, k + 1, *parts[p])
-        if k == 0:
-            net.wait(("az1+", p), at, me.dev(z=zm))
-            if p == 0:
-                net.send("af1+", at, a_at(q1, 3, *parts[p]), me.dev(z=zp))
-        elif k == 1:
-            net.wait(("az1-", p), at, me.dev(z=zp))
-            if p == 1:
-                net.send("af1-", at, a_at(q1, 3, *parts[p]), me.dev(z=zm))
-        elif p == 0:
-            net.wait("af1+", at, me.dev(z=zm))
-        else:
-            net.wait("af1-", at, me.dev(z=zp))
-        to_mate(k + 1, p)
-
-    def first_z1():
-        take_z1(0, 0)
-        take_z1(1, 1)
-
-    def ready_b(j):
-        last_x(j)
-        last_x(j + 4)
+    def sub(k, p, side_of):
+        first, size = parts[p]
+        upper = (size // 2 + 15) // 16 * 16
+        return a_at(q1, k, first, upper) if side_of == 0 else a_at(q1, k, first + upper, size - upper)
+
+    def take_z1(p):
+        net.wait(("az1+", p), a_at(q1, 1, *parts[p]), me.dev(z=zm))
+        net.send(("af1+", p), sub(1, p, 0), sub(3, p, 0), me.dev(z=zp))
+        net.wait(("az1-", p), a_at(q1, 2, *parts[p]), me.dev(z=zp))
+        net.send(("af1-", p), sub(2, p, 1), sub(3, p, 1), me.dev(z=zm))
+        to_mate(1, p)
+        to_mate(2, p)
+
+    def opposite_z1(p):
+        net.wait(("af1+", p), sub(3, p, 0), me.dev(z=zm))
+        net.wait(("af1-", p), sub(3, p, 1), me.dev(z=zp))
+        to_mate(3, p)
+
+    def ready_b(j, n):
+        last_x(j, n)
+        last_x(j + 4, n)
 
     def mate0():
         for k in range(4):
@@ -330,43 +335,49 @@
         for p in (0, 1, 2):
             net.need(("ac1", k, p), a_at((1 - yh) * 2 + 1 - core, k, *parts[p]), mate)
 
-    def units(yy, piece, first, count):
+    def units(yy, piece, n, first, count):
         zi = z_order[piece]
         deep = 4 * rows
         left = a[yy * 2 + zi // 2, pl.ds(first * rows, count * rows), pl.ds(pl.multiple_of((zi % 2) * deep, deep), deep)]
-        right = b[pl.ds(pl.multiple_of((yy * 4 + zi) * deep, deep), deep)]
-        c[pl.ds(first * rows, count * rows)] += jnp.dot(left, right, preferred_element_type=F32)
-
-    def early(j):
+        right = b[n, pl.ds(pl.multiple_of((yy * 4 + zi) * deep, deep), deep)]
+        c[pl.ds(first * rows, count * rows), n * side:(n + 1) * side] += jnp.dot(left, right, preferred_element_type=F32)
+
+    def early(j, n):
         mate0()
-        ready_b(j)
-        units(yh, j, 0, 4)
-
-    def late(j, first, count):
+        ready_b(j, n)
+        units(yh, j, n, 0, 4)
+
+    def late(j, n, first, count):
         for k in range(first, first + count):
             mate1(k)
-        ready_b(j)
-        units(1 - yh, j, first, count)
+        ready_b(j, n)
+        units(1 - yh, j, n, first, count)
 
     mine = yl * 4 + x
 
-    def finish(d):
+    def finish(d, n):
         zz = (z + d) % 4
         if d:
             net.need(("k", (4 - d) % 4), km.at[zz], me.dev(z=zz))
         slot = (0, 2, 3, 1)[d]
-        kept = c[slot * rows:(slot + 1) * rows] * km[zz, 0:1]
-        ts[mine] += jnp.sum(kept * kept, axis=0, keepdims=True)
+        at = slice(n * side, (n + 1) * side)
+        kept = c[slot * rows:(slot + 1) * rows, at] * km[zz, 0:1, at]
+        ts[mine, :, at] += jnp.sum(kept * kept, axis=0, keepdims=True)
         top = jnp.max(kept, axis=0, keepdims=True)
         up = jnp.where(top > 0, 32767.0 / jnp.where(top > 0, top, 1.0), 0.0)
-        cq[d] = jnp.round(kept * up).astype(jnp.int32).astype(jnp.int16)
-        gsend[d, :, :wide] = top * (1.0 / 32767.0)
+        cq[d, n] = jnp.round(kept * up).astype(jnp.int32).astype(jnp.int16)
+        gsend[d, :, at] = top * (1.0 / 32767.0)
         if d:
-            net.send(("c", d), cq.at[d], chunk(q_out, z), me.dev(z=zz))
+            net.send(("c", d, n), cq.at[d, n], half_chunk(q_out, z, n), me.dev(z=zz))
+
+    def finish_step(k, n):
+        for d in ((0,), (1, 3), (2,))[k]:
+            finish(d, n)
 
     def total():
-        own = pltpu.make_async_copy(cq.at[0], chunk(q_out, z), local_sem.at[0])
-        own.start()
+        own = [pltpu.make_async_copy(cq.at[0, n], half_chunk(q_out, z, n), local_sem.at[n]) for n in (0, 1)]
+        for copy in own:
+            copy.start()
         for d, dy in around:
             net.send(("t", d, dy), ts.at[mine], ts.at[mine], me.dev(x=(x + d) % 4, yl=(yl + dy) % 2))
         for d, dy in around:
@@ -379,41 +390,34 @@
         gs[z] = gsend[0]
         for d in (1, 3, 2):
             net.send(("s", d), gsend.at[d], gs.at[z], me.dev(z=(z + d) % 4))
-        own.wait()
+        for copy in own:
+            copy.wait()
         for d in (1, 3, 2):
             src = (z - d + 4) % 4
             net.wait(("s", d), gs.at[src], me.dev(z=src))
         gs_out[...] = gs[...]
         for d in (1, 3, 2):
             src = (z - d + 4) % 4
-            net.wait(("c", d), chunk(q_out, src), me.dev(z=src))
+            for n in (0, 1):
+                net.wait(("c", d, n), half_chunk(q_out, src, n), me.dev(z=src))
         net.drain()
 
-    def later_z1():
-        take_z1(0, 1)
-        take_z1(1, 0)
-
-    steps = {"start": start, "mx": masses_x, "inv": masses_z, "own": own_a, "nb0": own_b, "lx0": raw_x, "z0f": first_z0,
-             "z0a": middle_z0, "z0b": lambda: forward_z0(3), "z1a": first_z1, "tot": total}
-    for step in ORDER:
-        if step in steps:
-            steps[step]()
-        elif step == "z1b":
-            later_z1()
-        elif step == "z1c":
-            take_z1(2, 0)
-            take_z1(2, 1)
-        else:
-            {"home": home, "f": forward_x, "y": take_y, "fin": finish_z0, "r": take_rest, "E": early, "C": finish,
-             "L": lambda j: late(j, 0, 3), "O": lambda j: late(j, 3, 1)}[step[0]](step[1])
+    steps = {"start": start, "mx": masses_x, "inv": masses_z, "own": own_a, "nb0": own_b, "z1": take_z1, "zo": opposite_z1,
+             "tot": total, "home": home, "f": forward_x, "lx": raw_x, "sy": send_y, "sb": send_b, "sa": send_z0,
+             "g": forward_z0, "y": take_y, "fin": finish_z0, "r": take_rest, "E": early, "C": finish_step,
+             "L": lambda j, n: late(j, n, 0, 3), "O": lambda j, n: late(j, n, 3, 1)}
+    for name, *which in ORDER:
+        steps[name](*which)
+
 
 def body(flow, pattern, keep):
     rows, cols = flow.shape
     tile = cols // pattern.shape[1]
     wide = cols // 4
+    side = wide // 2
     vmem = pl.BlockSpec(memory_space=pltpu.VMEM)
     anyspace = pl.BlockSpec(memory_space=pl.ANY)
-    messages = 112
+    messages = 152
     coded, factors = pl.pallas_call(
         lambda *refs: kernel(tile, *refs),
         out_shape=(jax.ShapeDtypeStruct((rows, cols), jnp.int16), jax.ShapeDtypeStruct((4, 1, 2 * wide), F32)),
@@ -424,14 +428,14 @@
             pltpu.SMEM(pattern.shape, jnp.int32),
             pltpu.SMEM(keep.shape, jnp.int32),
             pltpu.VMEM((4, 4 * rows, cols), BF16),
-            pltpu.VMEM((32 * rows, wide), BF16),
+            pltpu.VMEM((2, 32 * rows, side), BF16),
             pltpu.VMEM((rows, cols), BF16),
             pltpu.VMEM((3, rows, cols), BF16),
             pltpu.VMEM((rows, cols), BF16),
-            pltpu.VMEM((3, rows, wide), BF16),
-            pltpu.VMEM((rows, wide), BF16),
+            pltpu.VMEM((3, 2, rows, side), BF16),
+            pltpu.VMEM((2, rows, side), BF16),
             pltpu.VMEM((4 * rows, wide), F32),
-            pltpu.VMEM((4, rows, wide), jnp.int16),
+            pltpu.VMEM((4, 2, rows, side), jnp.int16),
             pltpu.VMEM((4, 1, cols), F32),
             pltpu.VMEM((8, 1, cols), F32),
             pltpu.VMEM((2, 1, cols), F32),

time: 98.5 us -> 95.8 us (0.973)
  Pallas kernels: 96.5 us -> 93.8 us
    pallas_call x1, Pallas kernels: 96.5 us -> 93.8 us  [body(): pl.pallas_call(lambda *refs: kernel(tile, *refs), out_shape=(jax.ShapeDty...]
where the time goes in v5:
time: 95.8 us; the launch traced here: 95.7 us
  Pallas kernels  93.8 us (98%)
  other arithmetic  1.83 us (2%)
    pallas_call x1, Pallas kernels, body(): pl.pallas_call(lambda *refs: kernel(tile, *refs), out_shape=(jax.ShapeDty...  93.8 us

profile of v5, /device:TPU:0, one launch (start us, length us, event | category | flops | bytes accessed | tf_op | source)
XLA Modules:
  0.0 95.7 jit_solution(860799479192492567)
XLA Ops:
  0.0 93.8 %cluster.1 = (s16[256,2048]{1,0:T(8,128)(2,1)S(1)}, f32[4,1,1024]{2,1,0:T(1,128)S(1)}) custom-call(bf16[256,2048]{1,0:T(8,128)(2,1)} %refs_0_.1, s32[1,8]{1,0:T(1,128)} %refs_1_.1, s32[1,8]{1,0:T(1,128)} %refs_2_.1), custom_call_target="tpu_custom_call" | custom-call | tf_op jit(solution)/shard_map/cluster/pallas_call | solution.py:421
  93.9 1.8 %multiply_multiply_fusion = f32[256,2048]{1,0:T(8,128)} fusion(s16[256,2048]{1,0:T(8,128)(2,1)S(1)} %get-tuple-element.7, f32[2048]{0:T(1024)S(1)} %bitcast.3, f32[2048]{0:T(1024)S(1)} %bitcast.2), kind=kLoop, calls=%fused_computation | loop fusion | flops 2097152 | bytes 3162112 | tf_op jit(solution)/shard_map/mul | solution.py:458
  (1 shorter events, 0.0 us)

commit v6 on v5

--- a/solution.py
+++ b/solution.py
@@ -10,17 +10,17 @@
 BF16 = jnp.bfloat16
 RING = 7
 ORDER = (
-    ("start",), ("mx",), ("sb", 0), ("sb", 1), ("sy", 1), ("f", 0, 0), ("f", 0, 1), ("inv",), ("home", 4, 0),
-    ("home", 2, 1), ("g", 0), ("home", 1, 0), ("g", 1), ("own",), ("sa", 2), ("home", 4, 1), ("sa", 3),
-    ("home", 3, 1), ("sy", 0), ("y", 1), ("f", 1, 0), ("g", 2), ("home", 3, 0), ("home", 5, 0), ("f", 4, 1),
-    ("lx", 1), ("home", 2, 0), ("fin", 0), ("fin", 1), ("home", 7, 1), ("home", 1, 1), ("g", 3), ("lx", 0), ("sy", 2),
-    ("f", 7, 1), ("f", 2, 0), ("f", 5, 0), ("y", 0), ("f", 1, 1), ("nb0",), ("z1", 1), ("f", 4, 0), ("f", 3, 1),
-    ("home", 7, 0), ("fin", 2), ("f", 3, 0), ("r", 1), ("home", 6, 0), ("z1", 0), ("f", 7, 0), ("E", 1, 0),
-    ("home", 6, 1), ("E", 0, 0), ("E", 0, 1), ("f", 6, 0), ("r", 0), ("y", 2), ("E", 3, 1), ("home", 5, 1), ("zo", 1),
-    ("L", 1, 0), ("r", 2), ("L", 3, 0), ("f", 6, 1), ("E", 3, 0), ("L", 2, 0), ("L", 0, 0), ("f", 2, 1), ("zo", 0),
-    ("E", 2, 0), ("C", 1, 0), ("C", 0, 0), ("f", 5, 1), ("L", 3, 1), ("L", 0, 1), ("O", 2, 0), ("O", 1, 0),
-    ("O", 0, 0), ("O", 3, 0), ("C", 2, 0), ("O", 2, 1), ("O", 3, 1), ("O", 0, 1), ("E", 2, 1), ("O", 1, 1),
-    ("E", 1, 1), ("C", 2, 1), ("L", 2, 1), ("L", 1, 1), ("C", 0, 1), ("C", 1, 1), ("tot",),
+    ("start",), ("mx",), ("sa", 2), ("sb", 0), ("f", 0, 0), ("sb", 1), ("f", 0, 1), ("inv",), ("home", 2, 0),
+    ("home", 4, 0), ("home", 1, 1), ("sy", 1), ("g", 1), ("sa", 3), ("nb0",), ("home", 4, 1), ("sy", 0), ("own",),
+    ("f", 4, 0), ("g", 2), ("lx", 0), ("home", 6, 0), ("lx", 1), ("home", 1, 0), ("home", 3, 0), ("g", 0),
+    ("f", 2, 0), ("g", 3), ("sy", 2), ("home", 5, 1), ("fin", 1), ("y", 1), ("home", 2, 1), ("f", 1, 1), ("fin", 0),
+    ("f", 4, 1), ("fin", 2), ("f", 1, 0), ("y", 0), ("home", 5, 0), ("f", 3, 0), ("f", 6, 0), ("f", 5, 0), ("y", 2),
+    ("home", 7, 0), ("z1", 1), ("E", 2, 0), ("f", 5, 1), ("r", 1), ("home", 6, 1), ("E", 0, 1), ("z1", 0),
+    ("f", 7, 0), ("E", 1, 0), ("home", 3, 1), ("E", 1, 1), ("E", 0, 0), ("r", 0), ("f", 2, 1), ("f", 6, 1),
+    ("E", 3, 0), ("r", 2), ("zo", 1), ("L", 0, 0), ("home", 7, 1), ("L", 3, 0), ("L", 2, 0), ("L", 1, 0), ("f", 3, 1),
+    ("zo", 0), ("C", 1, 0), ("L", 1, 1), ("E", 2, 1), ("L", 0, 1), ("f", 7, 1), ("C", 0, 0), ("L", 2, 1), ("O", 0, 0),
+    ("O", 1, 0), ("O", 3, 0), ("O", 2, 0), ("C", 2, 0), ("O", 2, 1), ("O", 0, 1), ("E", 3, 1), ("L", 3, 1),
+    ("C", 1, 1), ("O", 3, 1), ("O", 1, 1), ("C", 2, 1), ("C", 0, 1), ("tot",),
 )
 
 

time: 95.8 us -> 95.1 us (level)
  no operation moved by 1% of the time
where the time goes in v6:
time: 95.1 us; the launch traced here: 95 us
  Pallas kernels  93.2 us (98%)
  other arithmetic  1.83 us (2%)
    pallas_call x1, Pallas kernels, body(): pl.pallas_call(lambda *refs: kernel(tile, *refs), out_shape=(jax.ShapeDty...  93.2 us

profile of v6, /device:TPU:0, one launch (start us, length us, event | category | flops | bytes accessed | tf_op | source)
XLA Modules:
  0.0 95.0 jit_solution(5624645978870581694)
XLA Ops:
  0.0 93.2 %cluster.1 = (s16[256,2048]{1,0:T(8,128)(2,1)S(1)}, f32[4,1,1024]{2,1,0:T(1,128)S(1)}) custom-call(bf16[256,2048]{1,0:T(8,128)(2,1)} %refs_0_.1, s32[1,8]{1,0:T(1,128)} %refs_1_.1, s32[1,8]{1,0:T(1,128)} %refs_2_.1), custom_call_target="tpu_custom_call" | custom-call | tf_op jit(solution)/shard_map/cluster/pallas_call | solution.py:421
  93.2 1.8 %multiply_multiply_fusion = f32[256,2048]{1,0:T(8,128)} fusion(s16[256,2048]{1,0:T(8,128)(2,1)S(1)} %get-tuple-element.7, f32[2048]{0:T(1024)S(1)} %bitcast.3, f32[2048]{0:T(1024)S(1)} %bitcast.2), kind=kLoop, calls=%fused_computation | loop fusion | flops 2097152 | bytes 3162112 | tf_op jit(solution)/shard_map/mul | solution.py:458
  (1 shorter events, 0.0 us)
